TPU v7x, 32 devices: a whole 2x2x4 slice. The times are simulated.
32 devices in a mesh: dp: 16 (over z, y, x), tensor: 2 (over core).
Axes of the slice: x: 2, y: 2, z: 4, core: 2. Of those that a mesh axis runs over, the one named last changes fastest.
Arguments:
- tokens: bfloat16 [2, 8192, 768], P(None, 'dp'), may hold values from -6 to 6
- seg_doc: int32 [2, 64], replicated, may hold values from 0 to 15, as said below
- doc_len: int32 [2, 16], replicated, may hold values from 1 to 1024, as said below
- w_qkv: bfloat16 [2, 3, 768, 768], P(None, None, None, 'tensor'), may hold values from -0.21875 to 0.21875
- b_qv: float32 [2, 2, 768], P(None, None, 'tensor'), may hold values from -3 to 3
- w_out: bfloat16 [2, 768, 768], P(None, 'tensor'), may hold values from -0.625 to 0.625
- w_up: bfloat16 [2, 768, 3072], P(None, None, 'tensor'), may hold values from -0.21875 to 0.21875
- b_up: float32 [2, 3072], P(None, 'tensor'), may hold values from -3 to 3
- w_down: bfloat16 [2, 3072, 768], P(None, 'tensor'), may hold values from -0.109375 to 0.109375
- norm_gain: float32 [2, 2, 768], replicated, may hold values from 0.25 to 1.75
- bias_terms: float32 [2, 4, 768], replicated, may hold values from -3 to 3
- seg_pos: float32 [8, 768], replicated, may hold values from -3 to 3
- cotangent: bfloat16 [2, 8192, 768], P(None, 'dp'), may hold values from -6 to 6
Outputs:
- encoded: bfloat16 [2, 8192, 768], P(None, 'dp')
- grad_tokens: float32 [2, 8192, 768], P(None, 'dp')
- grad_w_qkv: float32 [2, 3, 768, 768], P(None, None, 'dp', 'tensor')
- grad_b_qv: float32 [2, 2, 768], P(None, None, 'tensor')
- grad_w_out: float32 [2, 768, 768], P(None, 'tensor', 'dp')
- grad_w_up: float32 [2, 768, 3072], P(None, 'dp', 'tensor')
- grad_b_up: float32 [2, 3072], P(None, 'tensor')
- grad_w_down: float32 [2, 3072, 768], P(None, 'tensor', 'dp')
- grad_norm_gain: float32 [2, 2, 768], replicated
- grad_bias_terms: float32 [2, 4, 768], replicated
- grad_seg_pos: float32 [8, 768], replicated
Inputs may be any that keep to these rules, and one draw needn't show every extreme that they name: `seg_doc`: segment ids never fall along a micro-batch; every document 0 to 15 covers 1 to 8 consecutive segments. `doc_len`: A document of n segments has more than 128 * (n - 1) and at most 128 * n tokens; in every micro-batch one document has exactly 1024.
All inputs are finite; a program needn't handle non-finite values.
Results may differ from a plain program's by a relative error of at most 0.024.
Values may be sent and summed in bfloat16 or wider, within the bound.
A program may use at most 192 MiB of HBM per device.

v0:
```python
from functools import reduce

import jax
import jax.numpy as jnp
from jax import lax
from jax.sharding import PartitionSpec as P

HEAD_DIM = 64
SEG = 128
MAXSEG = 8


norm_eps = 1e-05
masked_score = -1e30


def norm_rows(values, gain, shift):
    centre = values - jnp.mean(values, axis=-1, keepdims=True)
    spread = jnp.mean(centre * centre, axis=-1, keepdims=True)
    return centre * lax.rsqrt(spread + norm_eps) * gain + shift


def exact_gelu(values):
    return jax.nn.gelu(values, approximate=False)


def my_rows(values):
    part_rows = values.shape[0] // lax.axis_size("tensor")
    return lax.dynamic_slice_in_dim(values, lax.axis_index("tensor") * part_rows, part_rows, 0)


def attn_scores(queries, key_rows, key_mask, split_shape):
    raw = jnp.einsum(
        "glhd,gmhd->ghlm",
        queries.reshape(split_shape),
        key_rows.reshape(split_shape),
        preferred_element_type=jnp.float32,
    ) * HEAD_DIM ** (-0.5)
    return jnp.where(key_mask[:, None, None, :], raw, masked_score)


def layer_forward(inputs, key_mask, weights):
    w_qkv, b_qv, w_out, w_up, b_up, w_down, norm_gain, bias_terms = weights
    groups, span = key_mask.shape
    row_count = inputs.shape[0]
    local_width = w_qkv.shape[2]
    split_shape = (groups, span, local_width // HEAD_DIM, HEAD_DIM)
    inputs_b = inputs.astype(jnp.bfloat16)
    projected = jnp.einsum("rd,cde->cre", inputs_b, w_qkv, preferred_element_type=jnp.float32)
    queries = (projected[0] + b_qv[0]).astype(jnp.bfloat16)
    key_rows = projected[1].astype(jnp.bfloat16)
    value_rows = (projected[2] + b_qv[1]).astype(jnp.bfloat16)
    scores = attn_scores(queries, key_rows, key_mask, split_shape)
    row_max = jnp.max(scores, axis=-1, keepdims=True)
    log_total = row_max + jnp.log(jnp.sum(jnp.exp(scores - row_max), axis=-1, keepdims=True))
    attn_probs = jnp.exp(scores - log_total).astype(jnp.bfloat16)
    head_out = jnp.einsum(
        "ghlm,gmhd->glhd",
        attn_probs,
        value_rows.reshape(split_shape),
        preferred_element_type=jnp.float32,
    )
    head_out = head_out.reshape(row_count, local_width).astype(jnp.bfloat16)
    attn_part = (
        lax.psum_scatter(
            jnp.dot(head_out, w_out, preferred_element_type=jnp.float32),
            "tensor",
            scatter_dimension=0,
            tiled=True,
        )
        + bias_terms[0]
    )
    resid_one = lax.all_gather(my_rows(inputs) + attn_part, "tensor", axis=0, tiled=True)
    hidden = norm_rows(resid_one, norm_gain[0], bias_terms[2])
    hidden_b = hidden.astype(jnp.bfloat16)
    pre_act = jnp.dot(hidden_b, w_up, preferred_element_type=jnp.float32) + b_up
    active_b = exact_gelu(pre_act).astype(jnp.bfloat16)
    mlp_part = (
        lax.psum_scatter(
            jnp.dot(active_b, w_down, preferred_element_type=jnp.float32),
            "tensor",
            scatter_dimension=0,
            tiled=True,
        )
        + bias_terms[1]
    )
    resid_two = lax.all_gather(my_rows(hidden) + mlp_part, "tensor", axis=0, tiled=True)
    stored = (
        inputs_b,
        queries,
        key_rows,
        value_rows,
        log_total,
        head_out,
        resid_one,
        hidden_b,
        pre_act,
        active_b,
        resid_two,
    )
    return (norm_rows(resid_two, norm_gain[1], bias_terms[3]), stored)


def layer_backward(grad_out, key_mask, weights, stored):
    w_qkv, b_qv, w_out, w_up, b_up, w_down, norm_gain, bias_terms = weights
    (
        inputs_b,
        queries,
        key_rows,
        value_rows,
        log_total,
        head_out,
        resid_one,
        hidden_b,
        pre_act,
        active_b,
        resid_two,
    ) = stored
    groups, span = key_mask.shape
    row_count, local_width = queries.shape
    split_shape = (groups, span, local_width // HEAD_DIM, HEAD_DIM)
    forward_two, norm_two = jax.vjp(norm_rows, resid_two, norm_gain[1], bias_terms[3])
    grad_two, gain_two, shift_two = norm_two(grad_out)
    grad_mlp = grad_two.astype(jnp.bfloat16)
    grad_wdown = jnp.dot(active_b.T, grad_mlp, preferred_element_type=jnp.float32)
    grad_act = jnp.dot(grad_mlp, w_down.T, preferred_element_type=jnp.float32)
    forward_gelu, gelu_back = jax.vjp(exact_gelu, pre_act)
    grad_pre = gelu_back(grad_act)[0].astype(jnp.bfloat16)
    grad_wup = jnp.dot(hidden_b.T, grad_pre, preferred_element_type=jnp.float32)
    up_part = lax.psum_scatter(
        jnp.dot(grad_pre, w_up.T, preferred_element_type=jnp.float32),
        "tensor",
        scatter_dimension=0,
        tiled=True,
    )
    grad_hidden = lax.all_gather(my_rows(grad_two) + up_part, "tensor", axis=0, tiled=True)
    forward_one, norm_one = jax.vjp(norm_rows, resid_one, norm_gain[0], bias_terms[2])
    grad_one, gain_one, shift_one = norm_one(grad_hidden)
    grad_attn = grad_one.astype(jnp.bfloat16)
    grad_wout = jnp.dot(head_out.T, grad_attn, preferred_element_type=jnp.float32)
    grad_heads = (
        jnp.dot(grad_attn, w_out.T, preferred_element_type=jnp.float32)
        .astype(jnp.bfloat16)
        .reshape(split_shape)
    )
    scores = attn_scores(queries, key_rows, key_mask, split_shape)
    attn_probs = jnp.exp(scores - log_total)
    grad_probs = jnp.einsum(
        "glhd,gmhd->ghlm",
        grad_heads,
        value_rows.reshape(split_shape),
        preferred_element_type=jnp.float32,
    )
    grad_values = jnp.einsum(
        "ghlm,glhd->gmhd",
        attn_probs.astype(jnp.bfloat16),
        grad_heads,
        preferred_element_type=jnp.float32,
    )
    grad_scores = (
        attn_probs * (grad_probs - jnp.sum(attn_probs * grad_probs, axis=-1, keepdims=True))
    ).astype(jnp.bfloat16)
    inv_root = HEAD_DIM ** (-0.5)
    grad_queries = (
        jnp.einsum(
            "ghlm,gmhd->glhd",
            grad_scores,
            key_rows.reshape(split_shape),
            preferred_element_type=jnp.float32,
        )
        * inv_root
    )
    grad_keys = (
        jnp.einsum(
            "ghlm,glhd->gmhd",
            grad_scores,
            queries.reshape(split_shape),
            preferred_element_type=jnp.float32,
        )
        * inv_root
    )
    grad_qkv = (
        jnp.stack([grad_queries, grad_keys, grad_values])
        .reshape(3, row_count, local_width)
        .astype(jnp.bfloat16)
    )
    grad_wqkv = jnp.einsum("rd,cre->cde", inputs_b, grad_qkv, preferred_element_type=jnp.float32)
    qkv_part = lax.psum_scatter(
        jnp.einsum("cre,cde->rd", grad_qkv, w_qkv, preferred_element_type=jnp.float32).astype(
            jnp.bfloat16
        ),
        "tensor",
        scatter_dimension=0,
        tiled=True,
    ).astype(jnp.float32)
    grad_inputs = lax.all_gather(
        (my_rows(grad_one) + qkv_part).astype(jnp.bfloat16), "tensor", axis=0, tiled=True
    ).astype(jnp.float32)
    grad_bqv = jnp.stack(
        [
            jnp.sum(grad_qkv[0].astype(jnp.float32), axis=0),
            jnp.sum(grad_qkv[2].astype(jnp.float32), axis=0),
        ]
    )
    grad_bup = jnp.sum(grad_pre.astype(jnp.float32), axis=0)
    grad_gain = jnp.stack([gain_one, gain_two])
    grad_shift = jnp.stack(
        [
            jnp.sum(grad_attn.astype(jnp.float32), axis=0),
            jnp.sum(grad_mlp.astype(jnp.float32), axis=0),
            shift_one,
            shift_two,
        ]
    )
    return (
        grad_inputs,
        (grad_wqkv, grad_bqv, grad_wout, grad_wup, grad_bup, grad_wdown, grad_gain, grad_shift),
    )


def deal_map(doc_ids, total_docs):
    return jnp.where(doc_ids % 2 == 1, (doc_ids + total_docs // 2) % total_docs, doc_ids)


def local_plan(seg_order, doc_lengths, seg_local, doc_local):
    total_docs = doc_lengths.shape[0]
    my_index = lax.axis_index("dp")
    doc_ids = jnp.arange(total_docs, dtype=jnp.int32)
    owner_pos = deal_map(doc_ids, total_docs)
    starts = jnp.sum((seg_order[None, :] < doc_ids[:, None]).astype(jnp.int32), axis=1)
    counts = jnp.sum((seg_order[None, :] == doc_ids[:, None]).astype(jnp.int32), axis=1)
    my_segments = my_index * seg_local + jnp.arange(seg_local, dtype=jnp.int32)
    seg_owner_doc = lax.dynamic_slice_in_dim(seg_order, my_index * seg_local, seg_local)
    seg_hot = seg_owner_doc[:, None] == doc_ids[None, :]
    my_start = jnp.sum(jnp.where(seg_hot, starts[None, :], 0), axis=1)
    my_length = jnp.sum(jnp.where(seg_hot, doc_lengths[None, :], 0), axis=1)
    my_owner = jnp.sum(jnp.where(seg_hot, owner_pos[None, :], 0), axis=1)
    within = my_segments - my_start
    valid_tokens = jnp.minimum(SEG, my_length - within * SEG)
    tok_mask = jnp.arange(SEG, dtype=jnp.int32)[None, :] < valid_tokens[:, None]
    src_slot = my_owner * MAXSEG + within
    my_deal = deal_map(my_index * doc_local + jnp.arange(doc_local, dtype=jnp.int32), total_docs)
    deal_hot = my_deal[:, None] == doc_ids[None, :]
    own_start = jnp.sum(jnp.where(deal_hot, starts[None, :], 0), axis=1)
    own_count = jnp.sum(jnp.where(deal_hot, counts[None, :], 0), axis=1)
    slot_index = jnp.arange(MAXSEG, dtype=jnp.int32)
    cross_mask = slot_index[None, :] < own_count[:, None]
    target = jnp.where(cross_mask, own_start[:, None] + slot_index[None, :], -1).reshape(-1)
    return (tok_mask, cross_mask, target, src_slot)


def picker(index_map, shard_rows):
    positions = jnp.arange(shard_rows.shape[0], dtype=jnp.int32)
    selector = (index_map[:, None] == positions[None, :]).astype(jnp.bfloat16)
    return jnp.dot(selector, shard_rows, preferred_element_type=jnp.float32)


def spreader(index_map, source_rows, row_span):
    positions = jnp.arange(row_span, dtype=jnp.int32)
    selector = (positions[:, None] == index_map[None, :]).astype(jnp.bfloat16)
    return jnp.dot(selector, source_rows, preferred_element_type=jnp.float32)


def add_terms(left, right):
    return jax.tree.map(jnp.add, left, right)


def local(
    tokens,
    seg_doc,
    doc_len,
    w_qkv,
    b_qv,
    w_out,
    w_up,
    b_up,
    w_down,
    norm_gain,
    bias_terms,
    seg_pos,
    cotangent,
):
    batches, local_rows, width = tokens.shape
    seg_local = local_rows // SEG
    doc_local = doc_len.shape[1] // lax.axis_size("dp")
    slot_rows = doc_local * MAXSEG

    def layer_weights(level):
        return (
            w_qkv[level],
            b_qv[level],
            w_out[level],
            w_up[level],
            b_up[level],
            w_down[level],
            norm_gain[level],
            bias_terms[level],
        )

    seg_weights = layer_weights(0)
    cross_weights = layer_weights(1)
    encoded = []
    grad_tokens = []
    seg_grads = []
    cross_grads = []
    pos_grads = []
    for batch_index in range(batches):
        tok_mask, cross_mask, target, src_slot = local_plan(
            seg_doc[batch_index], doc_len[batch_index], seg_local, doc_local
        )
        seg_out, seg_stored = layer_forward(
            tokens[batch_index].astype(jnp.float32), tok_mask, seg_weights
        )
        seg_cube = seg_out.reshape(seg_local, SEG, width)
        cls_rows = seg_cube[:, 0].astype(jnp.bfloat16)
        collected = picker(target, lax.all_gather(cls_rows, "dp", axis=0, tiled=True))
        cross_in = (collected.reshape(doc_local, MAXSEG, width) + seg_pos[None]).reshape(
            slot_rows, width
        )
        cross_out, cross_stored = layer_forward(cross_in, cross_mask, cross_weights)
        returned = picker(
            src_slot, lax.all_gather(cross_out.astype(jnp.bfloat16), "dp", axis=0, tiled=True)
        )
        encoded.append(
            seg_cube.at[:, 0].set(returned).reshape(local_rows, width).astype(jnp.bfloat16)
        )
        grad_cube = cotangent[batch_index].astype(jnp.float32).reshape(seg_local, SEG, width)
        grad_returned = grad_cube[:, 0].astype(jnp.bfloat16)
        grad_cross = lax.psum_scatter(
            spreader(src_slot, grad_returned, slot_rows * lax.axis_size("dp")),
            "dp",
            scatter_dimension=0,
            tiled=True,
        )
        grad_cross_in, cross_terms = layer_backward(
            grad_cross, cross_mask, cross_weights, cross_stored
        )
        pos_grads.append(jnp.sum(grad_cross_in.reshape(doc_local, MAXSEG, width), axis=0))
        grad_sent = grad_cross_in.astype(jnp.bfloat16)
        cross_grads.append(cross_terms)
        grad_cls = lax.psum_scatter(
            spreader(target, grad_sent, seg_local * lax.axis_size("dp")),
            "dp",
            scatter_dimension=0,
            tiled=True,
        )
        grad_seg = grad_cube.at[:, 0].set(grad_cls).reshape(local_rows, width)
        grad_inputs, seg_terms = layer_backward(grad_seg, tok_mask, seg_weights, seg_stored)
        grad_tokens.append(grad_inputs)
        seg_grads.append(seg_terms)
    seg_total = reduce(add_terms, seg_grads)
    cross_total = reduce(add_terms, cross_grads)
    pos_total = reduce(jnp.add, pos_grads)
    big_grads = (
        lax.psum_scatter(
            jnp.stack([seg_total[0], cross_total[0]]), "dp", scatter_dimension=2, tiled=True
        ),
        lax.psum_scatter(
            jnp.stack([seg_total[2], cross_total[2]]), "dp", scatter_dimension=2, tiled=True
        ),
        lax.psum_scatter(
            jnp.stack([seg_total[3], cross_total[3]]), "dp", scatter_dimension=1, tiled=True
        ),
        lax.psum_scatter(
            jnp.stack([seg_total[5], cross_total[5]]), "dp", scatter_dimension=2, tiled=True
        ),
    )
    small = lax.psum(
        (
            jnp.stack([seg_total[1], cross_total[1]]),
            jnp.stack([seg_total[4], cross_total[4]]),
            jnp.stack([seg_total[6], cross_total[6]]),
            jnp.stack([seg_total[7], cross_total[7]]),
            pos_total,
        ),
        "dp",
    )
    return (
        jnp.stack(encoded),
        jnp.stack(grad_tokens),
        big_grads[0],
        small[0],
        big_grads[1],
        big_grads[2],
        small[1],
        big_grads[3],
        small[2],
        small[3],
        small[4],
    )


def solution(mesh):
    in_specs = (
        P(None, "dp", None),
        P(),
        P(),
        P(None, None, None, "tensor"),
        P(None, None, "tensor"),
        P(None, "tensor", None),
        P(None, None, "tensor"),
        P(None, "tensor"),
        P(None, "tensor", None),
        P(),
        P(),
        P(),
        P(None, "dp", None),
    )
    out_specs = (
        P(None, "dp", None),
        P(None, "dp", None),
        P(None, None, "dp", "tensor"),
        P(None, None, "tensor"),
        P(None, "tensor", "dp"),
        P(None, "dp", "tensor"),
        P(None, "tensor"),
        P(None, "tensor", "dp"),
        P(),
        P(),
        P(),
    )
    return jax.shard_map(local, mesh=mesh, in_specs=in_specs, out_specs=out_specs, check_vma=False)
```

profile of v0, /device:TPU:0, one launch (start us, length us, event | category | flops | bytes accessed | tf_op | source)
XLA Modules:
  0.0 1395.4 jit_solution(11398153563986615864)
XLA Ops:
  8.1 2.8 fusion.71
  20.0 2.6 fusion.68
  34.8 11.1 reduce-scatter.12.cloned.1.call-done
  45.9 2.7 add_add_fusion.7
  49.5 10.3 all-gather.21.cloned.1.call-done
  62.0 10.8 all-gather.17.cloned.1.call-done
  76.7 11.5 multiply_convert_fusion.1
  89.4 2.6 fusion.34
  92.1 11.4 multiply_convert_fusion
  104.6 4.2 fusion.32
  108.9 10.3 reduce-scatter.18.cloned.1.call-done
  119.2 3.2 add_add_fusion.6
  139.7 6.4 all-gather.19.cloned.1.call-done
  151.9 42.1 %all-gather = bf16[64,1,768]{2,1,0:T(2,128)(2,1)S(1)} all-gather(bf16[4,1,768]{2,1,0:T(2,128)(2,1)S(1)} %slice.569), channel_id=2, replica_groups=mesh['dp'=16,'tensor'=2] {'dp'}, dimensions={0}, use_global_device_ids=true | all-gather | bytes 104448 | tf_op jit(solution)/shard_map/all_gather | solution.py:316
  194.6 36.6 %all-gather.1 = bf16[64,1,768]{2,1,0:T(2,128)(2,1)S(1)} all-gather(bf16[4,1,768]{2,1,0:T(2,128)(2,1)S(1)} %slice.567), channel_id=3, replica_groups=mesh['dp'=16,'tensor'=2] {'dp'}, dimensions={0}, use_global_device_ids=true | all-gather | bytes 104448 | tf_op jit(solution)/shard_map/all_gather | solution.py:316
  236.6 3.6 all-reduce.18
  254.0 4.2 all-reduce.17
  263.5 114.8 %reduce-scatter.26.cloned.1.call-done = f32[8,768]{1,0:T(8,128)} async-done(((f32[128,768]{1,0:T(8,128)}), f32[8,768]{1,0:T(8,128)}) %reduce-scatter.26.cloned.1.call-update) | async-done | bytes 24592 | tf_op jit(solution)/shard_map/reduce_scatter | solution.py:329
  382.1 3.0 convert_reduce_fusion.10
  388.1 3.0 convert_reduce_fusion.11
  393.5 4.1 all-reduce.16
  426.5 3.6 all-reduce.19
  441.1 101.3 %all-reduce.28.cloned.1.call-done = (f32[64,768]{1,0:T(8,128)}, f32[64,768]{1,0:T(8,128)}) async-done(((f32[64,768]{1,0:T(8,128)}, f32[64,768]{1,0:T(8,128)}), (f32[64,768]{1,0:T(8,128)}, f32[64,768]{1,0:T(8,128)})) %all-reduce.28.cloned.1.call-update) | async-done | bytes 393232
  547.1 4.5 fusion.75
  557.1 3.0 convert_reduce_fusion.1
  561.4 2.6 fusion.42
  566.4 6.6 convert_reduce_fusion
  574.2 4.3 fusion.40
  586.4 3.0 add_bitcast_fusion
  592.0 2.8 fusion.96
  594.8 3.2 fusion.330
  599.6 4.3 pad_maximum_fusion.1
  603.9 15.2 %copy.310 = f32[2,1536,768]{1,0,2:T(2,128)} copy(f32[2,1536,768]{2,1,0:T(8,128)} %pad_maximum_fusion.1) | data formatting | bytes 18874368 | tf_op jit(solution)/shard_map/stack | solution.py:365
  619.1 3.4 multiply_reduce_fusion.1
  622.6 2.7 fusion.339
  643.7 4.1 bitcast_convert_fusion.1
  661.0 3.7 bitcast_convert_fusion
  667.9 3.1 copy.309
  675.6 3.3 pad_maximum_fusion.2
  678.8 13.6 copy.308
  695.2 3.5 add_bitcast_fusion.2
  701.6 3.0 fusion.184
  704.7 3.6 add_bitcast_fusion.3
  711.0 8.4 pad_maximum_fusion
  720.2 41.6 %all_gather.71 = bf16[128,768]{1,0:T(8,128)(2,1)S(1)} all-gather(bf16[8,768]{1,0:T(8,128)(2,1)S(1)} %copy-done.136), channel_id=1, replica_groups=mesh['dp'=16,'tensor'=2] {'dp'}, dimensions={0}, use_global_device_ids=true | all-gather | bytes 208896 | tf_op jit(solution)/shard_map/all_gather | solution.py:322
  762.1 39.7 %all_gather.65 = bf16[128,768]{1,0:T(8,128)(2,1)S(1)} all-gather(bf16[8,768]{1,0:T(8,128)(2,1)S(1)} %copy-done.135), channel_id=1, replica_groups=mesh['dp'=16,'tensor'=2] {'dp'}, dimensions={0}, use_global_device_ids=true | all-gather | bytes 208896 | tf_op jit(solution)/shard_map/all_gather | solution.py:322
  812.3 456.9 %all-reduce.26.cloned.1.call-done = (f32[2,3,768,384]{3,0,1,2:T(2,128)}, f32[2,384,768]{1,0,2:T(2,128)}, f32[2,1536,768]{1,0,2:T(2,128)}) async-done(((f32[2,3,768,384]{3,0,1,2:T(2,128)}, f32[2,384,768]{1,0,2:T(2,128)}, f32[2,1536,768]{1,0,2:T(2,128)}), (f32[2,3,768,384]{3,0,1,2:T(2,128)}, f32[2,384,768]{1,0,2:T(2,128)}, f32[2,1536,768]{1,0,2:T(2,128)})) %all-reduce.26.cloned.1.call-update) | async-done | bytes 18874384
  1274.7 106.3 %all-reduce.24.cloned.1.call-done = (f32[2,2,384]{2,1,0:T(2,128)}, f32[2,1536]{1,0:T(2,128)}, f32[2,2,768]{2,1,0:T(2,128)}, f32[2,4,768]{2,1,0:T(4,128)}, f32[8,768]{1,0:T(8,128)}) async-done(((f32[2,2,384]{2,1,0:T(2,128)}, f32[2,1536]{1,0:T(2,128)}, f32[2,2,768]{2,1,0:T(2,128)}, f32[2,4,768]{2,1,0:T(4,128)}, f32[8,768]{1,0:T(8,128)}), (f32[2,2,384]{2,1,0:T(2,128)}, f32[2,1536]{1,0:T(2,128)}, ...) | async-done | bytes 79888 | tf_op jit(solution)/shard_map/psum | solution.py:368
  (869 shorter events, 221.8 us)
Async XLA Ops:
  8.0 26.8 %reduce-scatter.16.cloned.1.call-start = ((), (), s32[]{:S(2)}) async-start(), calls=%async_computation.15 | async-start | bytes 2359296 | tf_op jit(solution)/shard_map/reduce_scatter | solution.py:65
  14.6 14.7 %copy-start.100 = (f32[6,64]{1,0:T(8,128)}, f32[6,64]{1,0:T(8,128)S(1)}, u32[]{:S(2)}) copy-start(f32[6,64]{1,0:T(8,128)S(1)} %add.774) | copy-start | bytes 4612
  14.7 15.5 %copy-start.103 = (f32[6,64]{1,0:T(8,128)}, f32[6,64]{1,0:T(8,128)S(1)}, u32[]{:S(2)}) copy-start(f32[6,64]{1,0:T(8,128)S(1)} %add.768) | copy-start | bytes 4612
  20.0 25.9 %reduce-scatter.12.cloned.1.call-start = ((), (), s32[]{:S(2)}) async-start(), calls=%async_computation.11 | async-start | bytes 2359296 | tf_op jit(solution)/shard_map/reduce_scatter | solution.py:65
  34.0 25.8 %all-gather.21.cloned.1.call-start = ((), (), s32[]{:S(2)}) async-start(), calls=%async_computation.16 | async-start | bytes 2359296 | tf_op jit(solution)/shard_map/all_gather | solution.py:73
  48.6 24.1 %all-gather.17.cloned.1.call-start = ((), (), s32[]{:S(2)}) async-start(), calls=%async_computation.12 | async-start | bytes 2359296 | tf_op jit(solution)/shard_map/all_gather | solution.py:73
  49.2 59.7 %reduce-scatter.14.cloned.1.call-start = ((), (), s32[]{:S(2)}) async-start(), calls=%async_computation.13 | async-start | bytes 2359296 | tf_op jit(solution)/shard_map/reduce_scatter | solution.py:79
  62.0 14.7 %copy-start.138 = (f32[512]{0:T(512)}, f32[512]{0:T(512)S(1)}, u32[]{:S(2)}) copy-start(f32[512]{0:T(512)S(1)} %fusion.299) | copy-start | bytes 6148
  92.0 27.2 %reduce-scatter.18.cloned.1.call-start = ((), (), s32[]{:S(2)}) async-start(), calls=%async_computation.17 | async-start | bytes 2359296 | tf_op jit(solution)/shard_map/reduce_scatter | solution.py:79
  108.8 27.6 %all-gather.23.cloned.1.call-start = ((), (), s32[]{:S(2)}) async-start(), calls=%async_computation.18 | async-start | bytes 2359296 | tf_op jit(solution)/shard_map/all_gather | solution.py:87
  122.5 23.7 %all-gather.19.cloned.1.call-start = ((), (), s32[]{:S(2)}) async-start(), calls=%async_computation.14 | async-start | bytes 2359296 | tf_op jit(solution)/shard_map/all_gather | solution.py:87
  123.3 140.2 %reduce-scatter.20.cloned.1.call-start = ((), (), s32[]{:S(2)}) async-start(), calls=%async_computation.19 | async-start | bytes 417792 | tf_op jit(solution)/shard_map/reduce_scatter | solution.py:329
  127.8 250.5 %reduce-scatter.26.cloned.1.call-start = ((), (), s32[]{:S(2)}) async-start(), calls=%async_computation.23 | async-start | bytes 417792 | tf_op jit(solution)/shard_map/reduce_scatter | solution.py:329
  129.6 412.7 %all-reduce.28.cloned.1.call-start = ((), (), s32[]{:S(2)}) async-start(), calls=%async_computation.30 | async-start | bytes 786432
  132.4 98.8 %copy-start.198 = (s32[8]{0:T(128)}, s32[8]{0:T(128)S(1)}, u32[]{:S(2)}) copy-start(s32[8]{0:T(128)S(1)} %add_select_fusion) | copy-start | bytes 100
  135.0 59.0 %copy-start.200 = (s32[8]{0:T(128)}, s32[8]{0:T(128)S(1)}, u32[]{:S(2)}) copy-start(s32[8]{0:T(128)S(1)} %add_select_fusion.1) | copy-start | bytes 100
  149.6 44.3 %copy-start.109 = (f32[8,768]{1,0:T(8,128)S(1)}, f32[8,768]{1,0:T(8,128)}, u32[]{:S(2)}) copy-start(f32[8,768]{1,0:T(8,128)} %param.32) | copy-start | bytes 73732
  149.7 44.5 %copy-start.23 = (bf16[2,3,768,384]{3,2,1,0:T(8,128)(2,1)S(1)}, bf16[2,3,768,384]{3,2,1,0:T(8,128)(2,1)}, u32[]{:S(2)}) copy-start(bf16[2,3,768,384]{3,2,1,0:T(8,128)(2,1)} %param.24) | copy-start | bytes 10616836
  151.8 79.9 %copy-start.62 = (bf16[512,768]{1,0:T(8,128)(2,1)}, bf16[512,768]{1,0:T(8,128)(2,1)S(1)}, u32[]{:S(2)}) copy-start(bf16[512,768]{1,0:T(8,128)(2,1)S(1)} %get-tuple-element.224) | copy-start | bytes 2359300
  151.8 79.8 %copy-start.64 = (bf16[512,768]{1,0:T(8,128)(2,1)}, bf16[512,768]{1,0:T(8,128)(2,1)S(1)}, u32[]{:S(2)}) copy-start(bf16[512,768]{1,0:T(8,128)(2,1)S(1)} %get-tuple-element.225) | copy-start | bytes 2359300
  231.8 15.7 %copy-start.172 = (bf16[8,6,64]{2,1,0:T(8,128)(2,1)}, bf16[8,6,64]{2,1,0:T(8,128)(2,1)S(1)}, u32[]{:S(2)}) copy-start(bf16[8,6,64]{2,1,0:T(8,128)(2,1)S(1)} %convert_element_type.454) | copy-start | bytes 18436
  232.9 14.7 %copy-start.132 = (bf16[8,6,64]{2,1,0:T(8,128)(2,1)}, bf16[8,6,64]{2,1,0:T(8,128)(2,1)S(1)}, u32[]{:S(2)}) copy-start(bf16[8,6,64]{2,1,0:T(8,128)(2,1)S(1)} %get-tuple-element.250) | copy-start | bytes 18436
  251.8 127.9 %copy-start.168 = (f32[768]{0:T(1024)S(1)}, f32[768]{0:T(1024)}, u32[]{:S(2)}) copy-start(f32[768]{0:T(1024)} %get-tuple-element.123) | copy-start | bytes 9220
  403.4 20.7 %copy-start.94 = (f32[2,4,768]{2,1,0:T(4,128)}, f32[2,4,768]{2,1,0:T(4,128)S(1)}, u32[]{:S(2)}) copy-start(f32[2,4,768]{2,1,0:T(4,128)S(1)} %all-gather.8) | copy-start | bytes 73732
  435.5 143.0 %reduce-scatter.22.cloned.1.call-start = ((), (), s32[]{:S(2)}) async-start(), calls=%async_computation.20 | async-start | bytes 2359296 | tf_op jit(solution)/shard_map/reduce_scatter | solution.py:130
  438.5 108.6 %copy-start.128 = (f32[512]{0:T(512)S(1)}, f32[512]{0:T(512)}, u32[]{:S(2)}) copy-start(f32[512]{0:T(512)} %copy-done.127) | copy-start | bytes 6148
  438.5 108.6 %copy-start.130 = (f32[512]{0:T(512)S(1)}, f32[512]{0:T(512)}, u32[]{:S(2)}) copy-start(f32[512]{0:T(512)} %copy-done.129) | copy-start | bytes 6148
  438.5 108.6 %copy-start.143 = (f32[512]{0:T(512)S(1)}, f32[512]{0:T(512)}, u32[]{:S(2)}) copy-start(f32[512]{0:T(512)} %copy-done.142) | copy-start | bytes 6148
  438.5 108.5 %copy-start.145 = (f32[512]{0:T(512)S(1)}, f32[512]{0:T(512)}, u32[]{:S(2)}) copy-start(f32[512]{0:T(512)} %copy-done.144) | copy-start | bytes 6148
  564.0 25.4 %reduce-scatter.28.cloned.1.call-start = ((), (), s32[]{:S(2)}) async-start(), calls=%async_computation.24 | async-start | bytes 2359296 | tf_op jit(solution)/shard_map/reduce_scatter | solution.py:130
  578.5 40.6 %all-gather.25.cloned.1.call-start = ((), (), s32[]{:S(2)}) async-start(), calls=%async_computation.21 | async-start | bytes 2359296 | tf_op jit(solution)/shard_map/all_gather | solution.py:136
  580.9 38.1 %all-gather.27.cloned.1.call-start = ((), (), s32[]{:S(2)}) async-start(), calls=%async_computation.25 | async-start | bytes 2359296 | tf_op jit(solution)/shard_map/all_gather | solution.py:136
  591.8 211.6 %reduce-scatter.24.cloned.1.call-start = ((), (), s32[]{:S(2)}) async-start(), calls=%async_computation.22 | async-start | bytes 1179648 | tf_op jit(solution)/shard_map/reduce_scatter | solution.py:188
  603.8 15.2 %copy-start.124 = (f32[512]{0:T(512)S(1)}, f32[512]{0:T(512)}, u32[]{:S(2)}) copy-start(f32[512]{0:T(512)} %copy-done.123) | copy-start | bytes 6148
  603.8 15.2 %copy-start.126 = (f32[512]{0:T(512)S(1)}, f32[512]{0:T(512)}, u32[]{:S(2)}) copy-start(f32[512]{0:T(512)} %copy-done.125) | copy-start | bytes 6148
  603.8 15.2 %copy-start.139 = (f32[512]{0:T(512)S(1)}, f32[512]{0:T(512)}, u32[]{:S(2)}) copy-start(f32[512]{0:T(512)} %copy-done.138) | copy-start | bytes 6148
  603.9 15.2 %copy-start.141 = (f32[512]{0:T(512)S(1)}, f32[512]{0:T(512)}, u32[]{:S(2)}) copy-start(f32[512]{0:T(512)} %copy-done.140) | copy-start | bytes 6148
  626.0 38.8 %copy-start.13 = (f32[512,768]{1,0:T(8,128)}, f32[512,768]{1,0:T(8,128)S(1)}, u32[]{:S(2)}) copy-start(f32[512,768]{1,0:T(8,128)S(1)} %get-tuple-element.174) | copy-start | bytes 4718596
  647.7 159.2 %reduce-scatter.30.cloned.1.call-start = ((), (), s32[]{:S(2)}) async-start(), calls=%async_computation.26 | async-start | bytes 1179648 | tf_op jit(solution)/shard_map/reduce_scatter | solution.py:188
  664.8 604.4 %all-reduce.26.cloned.1.call-start = ((), (), s32[]{:S(2)}) async-start(), calls=%async_computation.29 | async-start | bytes 37748736
  692.6 688.4 %all-reduce.24.cloned.1.call-start = ((), (), s32[]{:S(2)}) async-start(), calls=%async_computation.28 | async-start | bytes 159744 | tf_op jit(solution)/shard_map/psum | solution.py:368
  711.0 670.1 %reduce-scatter.32.cloned.1.call-start = ((), (), s32[]{:S(2)}) async-start(), calls=%async_computation.27 | async-start | bytes 10027008 | tf_op jit(solution)/shard_map/reduce_scatter | solution.py:361
  719.4 42.4 %copy-start.203 = (s32[4]{0:T(128)S(1)}, s32[4]{0:T(128)}, u32[]{:S(2)}) copy-start(s32[4]{0:T(128)} %get-tuple-element.264) | copy-start | bytes 52
  719.4 42.6 %copy-start.65 = (bf16[512,768]{1,0:T(8,128)(2,1)S(1)}, bf16[512,768]{1,0:T(8,128)(2,1)}, u32[]{:S(2)}) copy-start(bf16[512,768]{1,0:T(8,128)(2,1)} %copy-done.64) | copy-start | bytes 2359300
  719.4 42.7 %copy-start.135 = (bf16[8,768]{1,0:T(8,128)(2,1)S(1)}, bf16[8,768]{1,0:T(8,128)(2,1)}, u32[]{:S(2)}) copy-start(bf16[8,768]{1,0:T(8,128)(2,1)} %get-tuple-element.219) | copy-start | bytes 36868
  719.4 82.4 %copy-start.205 = (s32[4]{0:T(128)S(1)}, s32[4]{0:T(128)}, u32[]{:S(2)}) copy-start(s32[4]{0:T(128)} %get-tuple-element.262) | copy-start | bytes 52
  719.4 82.6 %copy-start.63 = (bf16[512,768]{1,0:T(8,128)(2,1)S(1)}, bf16[512,768]{1,0:T(8,128)(2,1)}, u32[]{:S(2)}) copy-start(bf16[512,768]{1,0:T(8,128)(2,1)} %copy-done.62) | copy-start | bytes 2359300
  762.1 41.3 %copy-start.14 = (f32[512,768]{1,0:T(8,128)S(1)}, f32[512,768]{1,0:T(8,128)}, u32[]{:S(2)}) copy-start(f32[512,768]{1,0:T(8,128)} %copy-done.13) | copy-start | bytes 4718596
  (201 other events, 745.3 us)
Sparse Core Ops, SparseCore 0:
  20.1 11.7 reduce-scatter.15
  34.8 11.0 reduce-scatter.11
  48.8 10.9 all-gather.20
  61.8 10.9 all-gather.16
  92.1 10.2 reduce-scatter.13
  108.9 10.2 reduce-scatter.17
  122.6 10.9 all-gather.22
  135.2 10.9 all-gather.18
  564.1 8.0 reduce-scatter.21
  578.6 7.5 reduce-scatter.27
  587.8 10.9 all-gather.24
  600.3 10.9 all-gather.26
  647.9 6.6 reduce-scatter.23
  664.9 6.6 reduce-scatter.29
  719.6 353.3 reduce-scatter.31
Sparse Core Ops, SparseCore 1:
  129.0 122.9 reduce-scatter.19
  257.7 120.5 reduce-scatter.25
  435.6 106.7 all-reduce.27
  692.7 576.3 all-reduce.25
  1276.6 104.3 all-reduce.23
where the time goes:
time: 1410 us; the launch traced here: 1400 us
  waiting for transfers between devices  830 us (59%)
  blocking collectives  195 us (14%)
  matrix products  148 us (10%)
  local copies, waits for them, and re-layouts  103 us (7%)
  other arithmetic  96.4 us (7%)
  between operations  21.4 us (2%)
    unnamed x22, waiting for transfers between devices  560 us
    reduce_scatter x2, waiting for transfers between devices, local(): lax.psum_scatter(spreader(src_slot, grad_returned, slot_rows * lax.axis_s...  115 us
    psum x1, waiting for transfers between devices, local(): lax.psum((jnp.stack([seg_total[1], cross_total[1]]), jnp.stack([seg_total...  106 us
    all_gather x2, blocking collectives, local(): lax.all_gather(cross_out.astype(jnp.bfloat16), 'dp', axis=0, tiled=True)  81.2 us
    all_gather x2, blocking collectives, local(): lax.all_gather(cls_rows, 'dp', axis=0, tiled=True)  78.7 us
    unnamed x483, local copies, waits for them, and re-layouts  36.5 us
  transfers between devices with their start and end apart: 20, of which 9 were waited for; matrix products, arithmetic and copies ran while one was open for 14% of the time, Pallas kernels for 0%

commit v1 on v0

--- a/solution.py
+++ b/solution.py
@@ -1,8 +1,10 @@
-from functools import reduce
+from functools import partial, reduce
 
 import jax
 import jax.numpy as jnp
 from jax import lax
+from jax.experimental import pallas as pl
+from jax.experimental.pallas import tpu as pltpu
 from jax.sharding import PartitionSpec as P
 
 HEAD_DIM = 64
@@ -390,6 +392,1006 @@
     )
 
 
+BF = jnp.bfloat16
+F32 = jnp.float32
+D = 768
+FF = 3072
+HALF_FF = FF // 2
+HALF_D = D // 2
+CHUNK = 384
+CHUNKS = 12
+PAIRS = 6
+MESH = pl.DeviceIdType.MESH
+ROOT_HALF = 0.7071067811865476
+PDF_SCALE = 0.3989422804014327
+
+
+class Names:
+    def __init__(self, **kw):
+        self.__dict__.update(kw)
+
+
+def mm(left, right):
+    return jnp.dot(left, right, preferred_element_type=F32)
+
+
+def mm_nt(left, right):
+    return lax.dot_general(left, right, (((1,), (1,)), ((), ())), preferred_element_type=F32)
+
+
+def span(index, size):
+    return pl.ds(pl.multiple_of(index * size, size), size)
+
+
+def row_norm(rows):
+    centre = rows - jnp.mean(rows, axis=-1, keepdims=True)
+    spread = jnp.mean(centre * centre, axis=-1, keepdims=True)
+    scale = lax.rsqrt(spread + norm_eps)
+    return centre * scale, scale
+
+
+def stacked(pair, low_half):
+    zero = jnp.zeros_like(pair)
+    return jnp.concatenate(
+        [jnp.where(low_half, pair, zero), jnp.where(low_half, zero, pair)], axis=0
+    )
+
+
+def soft_rows(scores):
+    top = jnp.max(scores, axis=-1, keepdims=True)
+    grown = jnp.exp(scores - top)
+    return (grown * (1.0 / jnp.sum(grown, axis=-1, keepdims=True))).astype(BF)
+
+
+def transpose_into(dest, source, rows):
+    @pl.loop(0, rows // SEG)
+    def _(s):
+        dest[:, span(s, SEG)] = source[span(s, SEG), :].T
+
+
+def core_forward(r, keep, ready, y_block):
+    rows = r.xb.shape[0]
+    ready("qkv")
+
+    @pl.loop(0, 9)
+    def _(i):
+        c = lax.div(i, 3)
+        cols = span(lax.rem(i, 3), 256)
+        r.qkv[c, :, cols] = (mm(r.xb[...], r.wqkv[c, :, cols]) + r.b3[c, :, cols]).astype(BF)
+
+    @pl.loop(0, rows // SEG)
+    def _(s):
+        at = span(s, SEG)
+        live = keep(s)
+        low_half = lax.broadcasted_iota(jnp.int32, (SEG, SEG), 1) < HEAD_DIM
+        for p in range(PAIRS):
+            cols = slice(p * SEG, p * SEG + SEG)
+            keys = stacked(r.qkv[1, at, cols], low_half)
+            vals = stacked(r.qkv[2, at, cols], low_half)
+            raw = mm_nt(r.qkv[0, at, cols], keys) * HEAD_DIM ** (-0.5)
+            one = soft_rows(jnp.where(live, raw[:, :SEG], masked_score))
+            two = soft_rows(jnp.where(live, raw[:, SEG:], masked_score))
+            both = jnp.concatenate([one, two], axis=1)
+            r.p[s, p] = both
+            r.o[at, cols] = mm(both, vals).astype(BF)
+
+    ready("out")
+
+    @pl.loop(0, 3)
+    def _(n):
+        cols = span(n, 256)
+        r.xh1[:, cols] = mm(r.o[...], r.wout[:, cols]) + r.bt[0, :, cols]
+
+    @pl.loop(0, rows // 64)
+    def _(s):
+        at = span(s, 64)
+        hat, scale = row_norm(r.x_rows(at) + r.xh1[at, :])
+        r.xh1[at, :] = hat
+        r.rs1[at, :] = jnp.broadcast_to(scale, (64, SEG))
+        hidden = hat * r.gain[0] + r.bt[2]
+        r.h1[at, :] = hidden
+        r.h1b[at, :] = hidden.astype(BF)
+
+    ready("up")
+
+    @pl.loop(0, 12)
+    def _(j):
+        cols = span(j, 256)
+        for b in range(rows // SEG):
+            at = slice(b * SEG, b * SEG + SEG)
+            u = mm(r.h1b[at, :], r.wup[:, cols]) + r.bup[:, cols]
+            cdf = 0.5 * (1.0 + lax.erf(u * ROOT_HALF))
+            r.g[at, cols] = (u * cdf).astype(BF)
+            r.gp[at, cols] = (cdf + u * (PDF_SCALE * jnp.exp(-0.5 * u * u))).astype(BF)
+
+    transpose_into(r.h1t, r.h1b, rows)
+    ready("down")
+
+    @pl.loop(0, 3)
+    def _(n):
+        cols = span(n, 256)
+        r.xh2[:, cols] = r.h1[:, cols] + mm(r.g[...], r.wdown[:, cols]) + r.bt[1, :, cols]
+
+    @pl.loop(0, rows // 64)
+    def _(s):
+        at = span(s, 64)
+        hat, scale = row_norm(r.xh2[at, :])
+        r.xh2[at, :] = hat
+        r.rs2[at, :] = jnp.broadcast_to(scale, (64, SEG))
+        y_block(at, hat * r.gain[1] + r.bt[3])
+
+
+def norm_back(grad, hat, scale, gain):
+    d_hat = grad * gain
+    first = jnp.mean(d_hat, axis=-1, keepdims=True)
+    second = jnp.mean(d_hat * hat, axis=-1, keepdims=True)
+    return (d_hat - first - hat * second) * scale
+
+
+def norm_back_rows(r, rows, hat_ref, scale_ref, gain, grad_of):
+    zero = jnp.zeros((1, D), F32)
+
+    def step(s, sums):
+        at = span(s, 64)
+        grad = grad_of(s, at)
+        hat = hat_ref[at, :]
+        out = norm_back(grad, hat, scale_ref[at, 0:1], gain)
+        low = out.astype(BF)
+        r.dr[at, :] = out
+        r.dm[at, :] = low
+        return (
+            sums[0] + jnp.sum(grad * hat, axis=0, keepdims=True),
+            sums[1] + jnp.sum(grad, axis=0, keepdims=True),
+            sums[2] + jnp.sum(low.astype(F32), axis=0, keepdims=True),
+        )
+
+    sums = lax.fori_loop(0, rows // 64, step, (zero, zero, zero))
+    transpose_into(r.dmt, r.dm, rows)
+    return sums
+
+
+def core_backward(r, grad_of, ready, hooks):
+    rows = r.dr.shape[0]
+    ready("norm2")
+    sums = norm_back_rows(r, rows, r.xh2, r.rs2, r.gain[1], grad_of)
+    r.small_common[1], r.small_common[5], r.small_common[3] = sums
+    ready("down")
+    hooks("down")
+
+    @pl.loop(0, 12)
+    def _(j):
+        cols = span(j, 256)
+        total = jnp.zeros((1, 256), F32)
+        for b in range(rows // SEG):
+            at = slice(b * SEG, b * SEG + SEG)
+            du = (mm_nt(r.dm[at, :], r.wdown[cols, :]) * r.gp[at, cols].astype(F32)).astype(BF)
+            r.gp[at, cols] = du
+            total = total + jnp.sum(du.astype(F32), axis=0, keepdims=True)
+        r.bup_sum[:, cols] = total
+
+    hooks("up")
+    ready("up")
+
+    @pl.loop(0, 3)
+    def _(n):
+        cols = span(n, 256)
+        r.dr[:, cols] = r.dr[:, cols] + mm_nt(r.gp[...], r.wup[cols, :])
+
+    ready("norm1")
+    sums = norm_back_rows(r, rows, r.xh1, r.rs1, r.gain[0], lambda s, at: r.dr[at, :])
+    r.small_common[0], r.small_common[4], r.small_common[2] = sums
+    ready("out")
+    hooks("out")
+
+    @pl.loop(0, 3)
+    def _(n):
+        cols = span(n, 256)
+        r.o[:, cols] = mm_nt(r.dm[...], r.wout[cols, :]).astype(BF)
+
+    ready("attn")
+
+    @pl.loop(0, rows // SEG)
+    def _(s):
+        at = span(s, SEG)
+        low_half = lax.broadcasted_iota(jnp.int32, (SEG, SEG), 1) < HEAD_DIM
+        scale = HEAD_DIM ** (-0.5)
+        for p in range(PAIRS):
+            cols = slice(p * SEG, p * SEG + SEG)
+            query = r.qkv[0, at, cols]
+            keys = stacked(r.qkv[1, at, cols], low_half)
+            vals = stacked(r.qkv[2, at, cols], low_half)
+            d_head = r.o[at, cols]
+            probs = r.p[s, p]
+            d_probs = mm_nt(d_head, vals)
+            d_vals = mm(probs.T, d_head)
+            wide = probs.astype(F32)
+            prod = wide * d_probs
+            parts = []
+            for h in range(2):
+                own = slice(h * SEG, h * SEG + SEG)
+                parts.append(
+                    prod[:, own]
+                    - wide[:, own] * jnp.sum(prod[:, own], axis=-1, keepdims=True)
+                )
+            d_scores = jnp.concatenate(parts, axis=1).astype(BF)
+            d_keys = mm(d_scores.T, query) * scale
+            r.qkv[0, at, cols] = (mm(d_scores, keys) * scale).astype(BF)
+            r.qkv[1, at, cols] = jnp.where(low_half, d_keys[:SEG], d_keys[SEG:]).astype(BF)
+            r.qkv[2, at, cols] = jnp.where(low_half, d_vals[:SEG], d_vals[SEG:]).astype(BF)
+
+    for c in (0, 2):
+        r.qv_sum[c // 2] = jnp.sum(r.qkv[c].astype(F32), axis=0, keepdims=True)
+    ready("qkv")
+    hooks("qkv")
+
+    @pl.loop(0, 3)
+    def _(n):
+        cols = span(n, 256)
+        total = r.dr[:, cols]
+        for c in range(3):
+            total = total + mm_nt(r.qkv[c], r.wqkv[c, cols, :])
+        r.dr[:, cols] = total
+
+
+def chunk_operands(r, c):
+    if c < 4:
+        return r.dmt, (r.g, c * CHUNK, HALF_FF + c * CHUNK)
+    if c < 8:
+        return r.h1t, (r.gp, (c - 4) * CHUNK, HALF_FF + (c - 4) * CHUNK)
+    if c == 8:
+        return r.dmt, (r.o, 0, HALF_D)
+    return r.xt, (r.qkv.at[c - 9], 0, HALF_D)
+
+
+HOOK_CHUNKS = {"down": (0, 4), "up": (4, 8), "out": (8, 9), "qkv": (9, 12)}
+
+
+class Copies:
+    def __init__(self, sems):
+        self.sems = sems
+        self.used = 0
+
+    def start(self, source, dest):
+        copy = pltpu.make_async_copy(source, dest, self.sems.at[self.used])
+        self.used += 1
+        copy.start()
+        return copy
+
+
+def place():
+    return lax.axis_index("dp"), lax.axis_index("tensor")
+
+
+def remote(source, dest, send_sem, recv_sem, device):
+    return pltpu.make_async_remote_copy(
+        src_ref=source,
+        dst_ref=dest,
+        send_sem=send_sem,
+        recv_sem=recv_sem,
+        device_id=device,
+        device_id_type=MESH,
+    )
+
+
+def greet(devices):
+    barrier = pltpu.get_barrier_semaphore()
+    for device in devices:
+        pl.semaphore_signal(barrier, inc=1, device_id=device, device_id_type=MESH)
+    return barrier
+
+
+def load_half(copies, r, half, layer, wqkv, wout, wup, wdown, which):
+    if which == "qkv":
+        return copies.start(wqkv.at[layer], r.wqkv.at[:, :, half * HALF_D : (half + 1) * HALF_D])
+    if which == "out":
+        return copies.start(wout.at[layer], r.wout.at[half * HALF_D : (half + 1) * HALF_D, :])
+    if which == "up":
+        return copies.start(wup.at[layer], r.wup.at[:, half * HALF_FF : (half + 1) * HALF_FF])
+    return copies.start(wdown.at[layer], r.wdown.at[half * HALF_FF : (half + 1) * HALF_FF, :])
+
+
+def fill_bias(r, half, packed, layer):
+    lanes = slice(half * HALF_D, (half + 1) * HALF_D)
+    r.b3[0, :, lanes] = packed[layer, :, 0:HALF_D]
+    r.b3[1, :, lanes] = jnp.zeros((1, HALF_D), F32)
+    r.b3[2, :, lanes] = packed[layer, :, HALF_D : 2 * HALF_D]
+    r.bup[:, half * HALF_FF : (half + 1) * HALF_FF] = packed[layer, :, 2 * HALF_D :]
+
+
+WEIGHT_SCRATCH = dict(
+    wqkv=((3, D, D), BF), wout=((D, D), BF), wup=((D, FF), BF), wdown=((FF, D), BF)
+)
+PACK = 2 * HALF_D + HALF_FF
+
+
+def saved_shapes(rows):
+    return dict(
+        xt=((D, rows), BF),
+        h1t=((D, rows), BF),
+        qkv=((3, rows, D), BF),
+        o=((rows, D), BF),
+        p=((rows // SEG, PAIRS, SEG, 2 * SEG), BF),
+        xh1=((rows, D), F32),
+        rs1=((rows, SEG), F32),
+        g=((rows, FF), BF),
+        gp=((rows, FF), BF),
+        xh2=((rows, D), F32),
+        rs2=((rows, SEG), F32),
+    )
+
+
+def forward_shapes(rows):
+    return dict(
+        xb=((rows, D), BF),
+        h1=((rows, D), F32),
+        h1b=((rows, D), BF),
+        b3=((3, 1, D), F32),
+        bup=((1, FF), F32),
+    )
+
+
+def vmem(table):
+    return [pltpu.VMEM(shape, kind) for shape, kind in table.values()]
+
+
+def arrays(table):
+    return [jax.ShapeDtypeStruct(shape, kind) for shape, kind in table.values()]
+
+
+def first_kernel(dp, names, *refs):
+    r = Names(**dict(zip(names, refs)))
+    r.__dict__.update({k: getattr(r, "v_" + k) for k in saved_shapes(SEG)})
+    d, t = place()
+    sibling = (d, 1 - t)
+    rows = r.xb.shape[0]
+    segs = rows // SEG
+    barrier = greet([sibling] + [(lax.rem(d + o, dp), t) for o in range(1, dp)])
+    copies = Copies(r.local_sem)
+    own = (r.a_wqkv, r.a_wout, r.a_wup, r.a_wdown)
+    other = (r.x_wqkv, r.x_wout, r.x_wup, r.x_wdown)
+    load_x = copies.start(r.tokens.at[t], r.xb)
+    loads = {w: load_half(copies, r, 0, 0, *own, w) for w in ("qkv", "out", "up", "down")}
+    firsts = [copies.start(r.cot.at[t, pl.ds(s * SEG, 16)], r.cot_first.at[s]) for s in range(segs)]
+    pl.semaphore_wait(barrier, dp)
+    swaps = {}
+
+    def swap(layer, k):
+        swaps[layer, k] = remote(
+            own[k].at[layer], other[k].at[layer], r.w_send.at[layer, k], r.w_recv.at[layer, k], sibling
+        )
+        swaps[layer, k].start()
+
+    swap(0, 0)
+    swap_bias = remote(r.packed, r.x_packed, r.w_send.at[0, 4], r.w_recv.at[0, 4], sibling)
+    swap_bias.start()
+    swap(0, 1)
+    for copy in firsts:
+        copy.wait()
+
+    def gather(own_rows, everyone, send, recv):
+        everyone[d] = own_rows
+        sends = []
+        for o in range(1, dp):
+            copy = remote(
+                everyone.at[d], everyone.at[d], send.at[o], recv.at[d], (lax.rem(d + o, dp), t)
+            )
+            copy.start()
+            sends.append(copy)
+        return sends
+
+    def arrived(everyone, send, recv):
+        for o in range(1, dp):
+            source = lax.rem(d + o, dp)
+            remote(everyone.at[source], everyone.at[source], send.at[o], recv.at[source], (source, t)).wait_recv()
+
+    cot_rows = jnp.concatenate([r.cot_first[s].astype(F32)[0:1] for s in range(segs)], axis=0)
+    sends = gather(cot_rows.astype(BF), r.cot_all, r.cot_send, r.cot_recv)
+
+    def ready(phase):
+        if phase == "qkv":
+            load_x.wait()
+            transpose_into(r.xt, r.xb, rows)
+            fill_bias(r, 0, r.packed, 0)
+            loads["qkv"].wait()
+            swaps[0, 0].wait_recv()
+            more = load_half(copies, r, 1, 0, *other, "qkv")
+            swap(0, 2)
+            swap(0, 3)
+            swap_bias.wait_recv()
+            fill_bias(r, 1, r.x_packed, 0)
+            more.wait()
+        else:
+            k = {"out": 1, "up": 2, "down": 3}[phase]
+            swaps[0, k].wait_recv()
+            more = load_half(copies, r, 1, 0, *other, phase)
+            if phase == "out":
+                for w in range(4):
+                    swap(1, w)
+            loads[phase].wait()
+            more.wait()
+
+    def keep(s):
+        seg = d * segs + s
+        doc = r.seg_doc[t, seg]
+        within = jnp.int32(0)
+        for back in range(1, MAXSEG):
+            same = r.seg_doc[t, jnp.maximum(seg - back, 0)] == doc
+            within = within + jnp.where(jnp.logical_and(seg >= back, same), 1, 0)
+        valid = jnp.minimum(SEG, r.doc_len[t, doc] - SEG * within)
+        return lax.broadcasted_iota(jnp.int32, (1, SEG), 1) < valid
+
+    r.x_rows = lambda at: r.xb[at, :].astype(F32)
+
+    def y_block(at, values):
+        r.v_y1[at, :] = values.astype(BF)
+
+    core_forward(r, keep, ready, y_block)
+    cls = jnp.concatenate(
+        [r.v_y1[s * SEG : s * SEG + 16, :].astype(F32)[0:1] for s in range(segs)], axis=0
+    )
+    sends += gather(cls.astype(BF), r.cls_all, r.cls_send, r.cls_recv)
+    outs = [copies.start(getattr(r, "v_" + k), getattr(r, "o_" + k)) for k in list(saved_shapes(SEG)) + ["y1"]]
+    outs.append(copies.start(r.x_packed, r.o_packed))
+    arrived(r.cot_all, r.cot_send, r.cot_recv)
+    outs.append(copies.start(r.cot_all, r.o_cot))
+    arrived(r.cls_all, r.cls_send, r.cls_recv)
+    outs.append(copies.start(r.cls_all, r.o_cls))
+    for copy in sends:
+        copy.wait_send()
+    swap_bias.wait_send()
+    for (layer, k), copy in swaps.items():
+        copy.wait_send()
+        if layer == 1:
+            copy.wait_recv()
+    for copy in outs:
+        copy.wait()
+
+
+def run_first(dp, rows, seg_doc, doc_len, tokens, cot, packed, gain, terms, wqkv, wout, wup, wdown):
+    hbm = pl.BlockSpec(memory_space=pl.ANY)
+    smem = pl.BlockSpec(memory_space=pltpu.SMEM)
+    small = pl.BlockSpec(memory_space=pltpu.VMEM)
+    segs = rows // SEG
+    saved = saved_shapes(rows)
+    outs = dict(
+        x_wqkv=(wqkv.shape, BF),
+        x_wout=(wout.shape, BF),
+        x_wup=(wup.shape, BF),
+        x_wdown=(wdown.shape, BF),
+        o_packed=(packed.shape, F32),
+        o_cls=((dp, segs, D), BF),
+        o_cot=((dp, segs, D), BF),
+        o_y1=((rows, D), BF),
+    )
+    outs.update({"o_" + k: v for k, v in saved.items()})
+    scratch = {"v_" + k: v for k, v in saved.items()}
+    scratch["v_y1"] = ((rows, D), BF)
+    scratch.update(WEIGHT_SCRATCH)
+    scratch.update(forward_shapes(rows))
+    scratch.update(
+        x_packed=(packed.shape, F32),
+        cls_all=((dp, segs, D), BF),
+        cot_all=((dp, segs, D), BF),
+        cot_first=((segs, 16, D), BF),
+    )
+    sems = dict(
+        local_sem=pltpu.SemaphoreType.DMA((40,)),
+        w_send=pltpu.SemaphoreType.DMA((2, 5)),
+        w_recv=pltpu.SemaphoreType.DMA((2, 5)),
+        cot_send=pltpu.SemaphoreType.DMA((dp,)),
+        cot_recv=pltpu.SemaphoreType.DMA((dp,)),
+        cls_send=pltpu.SemaphoreType.DMA((dp,)),
+        cls_recv=pltpu.SemaphoreType.DMA((dp,)),
+    )
+    ins = ["seg_doc", "doc_len", "tokens", "cot", "packed", "gain", "bt", "a_wqkv", "a_wout", "a_wup", "a_wdown"]
+    names = ins + list(outs) + list(scratch) + list(sems)
+    result = pl.pallas_call(
+        partial(first_kernel, dp, names),
+        out_shape=arrays(outs),
+        in_specs=[smem, smem, hbm, hbm, small, small, small, hbm, hbm, hbm, hbm],
+        out_specs=[hbm] * len(outs),
+        scratch_shapes=vmem(scratch) + list(sems.values()),
+        compiler_params=pltpu.CompilerParams(
+            collective_id=0, has_side_effects=True, vmem_limit_bytes=60 << 20
+        ),
+        name="segment_forward",
+    )(seg_doc, doc_len, tokens, cot, packed, gain, terms, wqkv, wout, wup, wdown)
+    return dict(zip(outs, result))
+
+
+def cross_kernel(segs, names, *refs):
+    r = Names(**dict(zip(names, refs)))
+    d, t = place()
+    total_segs = r.cls.shape[0]
+    slots = r.dr.shape[0]
+    total_docs = slots // MAXSEG
+    copies = Copies(r.local_sem)
+    own = (r.a_wqkv, r.a_wout, r.a_wup, r.a_wdown)
+    other = (r.x_wqkv, r.x_wout, r.x_wup, r.x_wdown)
+    loads = {}
+    for which in ("qkv", "out", "up", "down"):
+        loads[which] = [
+            load_half(copies, r, half, 1, *source, which) for half, source in enumerate((own, other))
+        ]
+
+    def ready(phase):
+        for copy in loads.pop(phase, ()):
+            copy.wait()
+
+    fill_bias(r, 0, r.packed, 1)
+    fill_bias(r, 1, r.x_packed, 1)
+
+    doc_row = jnp.broadcast_to(r.seg_doc[t], (total_segs, total_segs))
+    below = lax.broadcasted_iota(jnp.int32, (total_segs, total_segs), 0)
+    across = lax.broadcasted_iota(jnp.int32, (total_segs, total_segs), 1)
+    doc_col = jnp.sum(jnp.where(below == across, doc_row, 0).astype(F32), axis=1, keepdims=True)
+    earlier = jnp.logical_and(doc_col == doc_row.astype(F32), below < across)
+    within = jnp.sum(jnp.where(earlier, 1.0, 0.0), axis=0, keepdims=True).astype(jnp.int32)
+    doc = r.seg_doc[t]
+    moved = doc + total_docs // 2
+    moved = jnp.where(moved >= total_docs, moved - total_docs, moved)
+    slot_of = jnp.where((doc & 1) == 1, moved, doc) * MAXSEG + within
+    slot_ids = lax.broadcasted_iota(jnp.int32, (slots, total_segs), 0)
+    deal = jnp.where(slot_ids == slot_of, 1.0, 0.0).astype(BF)
+    pick_row = lax.broadcasted_iota(jnp.int32, (8, total_segs), 0)
+    pick_seg = lax.broadcasted_iota(jnp.int32, (8, total_segs), 1)
+    pick = jnp.where(
+        jnp.logical_and(pick_row < segs, pick_seg == d * segs + pick_row), 1.0, 0.0
+    ).astype(BF)
+    back = mm_nt(pick, deal).astype(BF)
+    live = mm_nt(jnp.ones((8, total_segs), BF), deal)[0:1] > 0.5
+    key_doc = lax.broadcasted_iota(jnp.int32, (SEG, SEG), 1) >> 3
+    row_doc = lax.broadcasted_iota(jnp.int32, (SEG, SEG), 0) >> 3
+    allowed = jnp.logical_and(key_doc == row_doc, live)
+
+    r.x32[...] = mm(deal, r.cls[...]) + jnp.concatenate([r.pos[...]] * total_docs, axis=0)
+    r.xb[...] = r.x32[...].astype(BF)
+    r.dy[...] = mm(deal, r.cot[...])
+    r.x_rows = lambda at: r.x32[at, :]
+    transpose_into(r.xt, r.xb, slots)
+
+    def y_block(at, values):
+        r.yb[at, :] = values.astype(BF)
+
+    core_forward(r, lambda s: allowed, ready, y_block)
+    r.ret[...] = mm(back, r.yb[...])
+    shard = D // r.dp
+
+    def hooks(name):
+        low, high = HOOK_CHUNKS[name]
+        for c in range(low, high):
+            left, (right, own_at, other_at) = chunk_operands(r, c)
+            mine = left[pl.ds(pl.multiple_of(d * shard, 16), shard), :]
+            r.shard[0, c] = mm(mine, right[:, own_at : own_at + CHUNK])
+            r.shard[1, c] = mm(mine, right[:, other_at : other_at + CHUNK])
+
+    r.small_common = r.small
+    core_backward(r, lambda s, at: r.dy[at, :], ready, hooks)
+    pack_halves(r)
+    low = r.dr[...].astype(BF)
+    r.dc[...] = mm(back, low)
+    total = r.dr[0:MAXSEG, :]
+    for j in range(1, total_docs):
+        total = total + r.dr[j * MAXSEG : (j + 1) * MAXSEG, :]
+    r.d_pos[...] = total
+
+
+def pack_halves(r):
+    for half in range(2):
+        at = 6 + 3 * half
+        lanes = slice(half * HALF_D, (half + 1) * HALF_D)
+        r.small[at, :, 0:HALF_D] = r.qv_sum[0, :, lanes]
+        r.small[at, :, HALF_D:] = r.qv_sum[1, :, lanes]
+        base = half * HALF_FF
+        r.small[at + 1] = r.bup_sum[:, base : base + D]
+        r.small[at + 2] = r.bup_sum[:, base + D : base + 2 * D]
+
+
+BACK_SCRATCH = dict(qv_sum=((2, 1, D), F32), bup_sum=((1, FF), F32))
+
+
+def run_cross(dp, segs, slots, seg_doc, cls, cot, pos, packed, x_packed, gain, terms, own, other):
+    hbm = pl.BlockSpec(memory_space=pl.ANY)
+    small = pl.BlockSpec(memory_space=pltpu.VMEM)
+    outs = dict(
+        ret=((8, D), F32),
+        dc=((8, D), F32),
+        d_pos=((MAXSEG, D), F32),
+        small=((12, 1, D), F32),
+        shard=((2, CHUNKS, D // dp, CHUNK), F32),
+    )
+    scratch = dict(saved_shapes(slots))
+    scratch.update(WEIGHT_SCRATCH)
+    scratch.update(forward_shapes(slots))
+    scratch.update(BACK_SCRATCH)
+    scratch.update(
+        x32=((slots, D), F32),
+        dy=((slots, D), F32),
+        yb=((slots, D), BF),
+        dr=((slots, D), F32),
+        dm=((slots, D), BF),
+        dmt=((D, slots), BF),
+    )
+    ins = ["seg_doc", "cls", "cot", "pos", "packed", "x_packed", "gain", "bt"]
+    ins += ["a_wqkv", "a_wout", "a_wup", "a_wdown", "x_wqkv", "x_wout", "x_wup", "x_wdown"]
+    names = ins + list(outs) + list(scratch) + ["local_sem"]
+
+    def kernel(*refs):
+        cross_kernel_with(dp, segs, names, *refs)
+
+    result = pl.pallas_call(
+        kernel,
+        out_shape=arrays(outs),
+        in_specs=[small] * 8 + [hbm] * 8,
+        out_specs=[small] * len(outs),
+        scratch_shapes=vmem(scratch) + [pltpu.SemaphoreType.DMA((8,))],
+        compiler_params=pltpu.CompilerParams(vmem_limit_bytes=60 << 20),
+        name="document_layer",
+    )(seg_doc, cls, cot, pos, packed, x_packed, gain, terms, *own, *other)
+    return dict(zip(outs, result))
+
+
+def cross_kernel_with(dp, segs, names, *refs):
+    cross_kernel(segs, names + ["dp"], *refs, dp)
+
+
+SLOTS = 4
+
+
+def last_kernel(dp, names, *refs):
+    r = Names(**dict(zip(names, refs)))
+    d, t = place()
+    x, y, z = lax.rem(d, 2), lax.rem(lax.div(d, 2), 2), lax.div(d, 4)
+    zs = dp // 4
+    sibling = (d, 1 - t)
+
+    def chip(x_at, y_at, z_at):
+        return (z_at * 4 + y_at * 2 + x_at, t)
+
+    x_peer, y_peer = chip(1 - x, y, z), chip(x, 1 - y, z)
+    z_peers = [chip(x, y, lax.rem(z + o, zs)) for o in range(1, zs)]
+    barrier = greet([sibling, x_peer, y_peer] + z_peers)
+    copies = Copies(r.local_sem)
+    own = (r.a_wqkv, r.a_wout, r.a_wup, r.a_wdown)
+    other = (r.x_wqkv, r.x_wout, r.x_wup, r.x_wdown)
+    loads = {}
+
+    def load(phase, *keys):
+        loads.setdefault(phase, []).extend(
+            copies.start(getattr(r, "i_" + k), getattr(r, k)) for k in keys
+        )
+
+    def load_weight(phase, which):
+        for half, source in enumerate((own, other)):
+            loads.setdefault(phase, []).append(load_half(copies, r, half, 0, *source, which))
+
+    loads["norm2"] = [copies.start(r.i_cot.at[t], r.cot)]
+    load("norm2", "xh2", "rs2")
+    load("down", "g")
+    load_weight("down", "down")
+    load("down", "gp", "h1t")
+    load_weight("up", "up")
+    load("norm1", "xh1", "rs1")
+    load("out", "o")
+    load_weight("out", "out")
+    load("attn", "qkv", "p")
+    load("qkv", "xt")
+    load_weight("qkv", "qkv")
+    load("enc", "y1")
+    load("shard", "shard1")
+
+    def ready(phase):
+        for copy in loads.pop(phase, ()):
+            copy.wait()
+
+    pl.semaphore_wait(barrier, zs + 2)
+    shard_swap = remote(r.i_shard1.at[1], r.shard_in, r.misc_send.at[0], r.misc_recv.at[0], sibling)
+    shard_swap.start()
+    small1_swap = [
+        remote(r.small1.at[0:6], r.small1_in.at[0:6], r.misc_send.at[1], r.misc_recv.at[1], sibling),
+        remote(r.small1.at[9:20], r.small1_in.at[6:17], r.misc_send.at[2], r.misc_recv.at[2], sibling),
+    ]
+    for copy in small1_swap:
+        copy.start()
+
+    first_row = lax.broadcasted_iota(jnp.int32, (64, 1), 0)
+
+    def with_first(values, s, table):
+        row = first_row + 64 * lax.rem(s, 2)
+        return jnp.where(row == 0, table[lax.div(s, 2)], values)
+
+    def sib_copy(c):
+        slot = lax.rem(c, SLOTS)
+        return remote(
+            r.sib_out.at[slot], r.sib_in.at[slot], r.sib_send.at[slot], r.sib_recv.at[slot], sibling
+        )
+
+    def stage_one(c, even):
+        source = r.gbuf.at[c, :, :, 1 - x] if even else r.gbuf.at[c, :, 1 - y]
+        return remote(source, r.one_in.at[c], r.one_send.at[c], r.one_recv.at[c], x_peer if even else y_peer)
+
+    def stage_two(c, even):
+        source = r.gbuf.at[c, :, 1 - y, x] if even else r.gbuf.at[c, :, y, 1 - x]
+        return remote(source, r.two_in.at[c], r.two_send.at[c], r.two_recv.at[c], y_peer if even else x_peer)
+
+    def stage_three(c, o):
+        return remote(
+            r.gbuf.at[c, lax.rem(z + o, zs), y, x],
+            r.three_in.at[c, o - 1],
+            r.three_send.at[c, o - 1],
+            r.three_recv.at[c, o - 1],
+            z_peers[o - 1],
+        )
+
+    def by_parity(c, act):
+        @pl.when(lax.rem(c, 2) == 0)
+        def _():
+            act(True)
+
+        @pl.when(lax.rem(c, 2) == 1)
+        def _():
+            act(False)
+
+    def progress(c):
+        sib_copy(c).wait_recv()
+        slot = lax.rem(c, SLOTS)
+        r.gbuf[c] = r.gbuf[c] + r.sib_in[slot].reshape(zs, 2, 2, D // dp, CHUNK)
+
+        @pl.when(c < CHUNKS - SLOTS)
+        def _():
+            pl.semaphore_signal(r.credit, inc=1, device_id=sibling, device_id_type=MESH)
+
+        by_parity(c, lambda even: stage_one(c, even).start())
+
+    def emit(c, left, right, own_at, other_at):
+        @pl.when(c >= SLOTS)
+        def _():
+            sib_copy(c).wait_send()
+            pl.semaphore_wait(r.credit, 1)
+
+        slot = lax.rem(c, SLOTS)
+        r.sib_out[slot] = mm(left[...], right[:, pl.ds(other_at, CHUNK)]).astype(BF)
+        sib_copy(c).start()
+        mine = mm(left[...], right[:, pl.ds(own_at, CHUNK)]).astype(BF)
+        r.gbuf[c] = mine.reshape(zs, 2, 2, D // dp, CHUNK)
+
+        @pl.when(c >= 1)
+        def _():
+            progress(c - 1)
+
+    def hooks(name):
+        low, high = HOOK_CHUNKS[name]
+        if name == "out":
+            emit(jnp.int32(8), r.dmt, r.o, 0, HALF_D)
+            return
+
+        @pl.loop(low, high)
+        def _(c):
+            if name == "qkv":
+                emit(c, r.xt, r.qkv.at[c - low], 0, HALF_D)
+            else:
+                base = pl.multiple_of((c - low) * CHUNK, 128)
+                left, right = (r.dmt, r.g) if name == "down" else (r.h1t, r.gp)
+                emit(c, left, right, base, pl.multiple_of(base + HALF_FF, 128))
+
+    r.small_common = r.small
+    core_backward(
+        r, lambda s, at: with_first(r.cot[at, :].astype(F32), s, r.dc), ready, hooks
+    )
+    progress(jnp.int32(CHUNKS - 1))
+    pack_halves(r)
+    small_swap = [
+        remote(r.small.at[0:6], r.small_in.at[0:6], r.misc_send.at[3], r.misc_recv.at[3], sibling),
+        remote(r.small.at[9:12], r.small_in.at[6:9], r.misc_send.at[4], r.misc_recv.at[4], sibling),
+    ]
+    for copy in small_swap:
+        copy.start()
+    grad_swap = remote(r.dr, r.o_grad.at[t], r.misc_send.at[5], r.misc_recv.at[5], sibling)
+    grad_swap.start()
+    outs = [copies.start(r.dr, r.o_grad.at[t])]
+    ready("enc")
+
+    @pl.loop(0, r.y1.shape[0] // 64)
+    def _(s):
+        at = span(s, 64)
+        r.y1[at, :] = with_first(r.y1[at, :].astype(F32), s, r.ret).astype(BF)
+
+    enc_swap = remote(r.y1, r.o_enc.at[t], r.misc_send.at[6], r.misc_recv.at[6], sibling)
+    enc_swap.start()
+    outs.append(copies.start(r.y1, r.o_enc.at[t]))
+    for copy in small_swap:
+        copy.wait()
+    r.total[...] = r.small[0:9] + r.small_in[...]
+    x_small = remote(r.total, r.x_small, r.misc_send.at[7], r.misc_recv.at[7], x_peer)
+    x_small.start()
+
+    @pl.loop(0, CHUNKS)
+    def _(c):
+        def act(even):
+            stage_one(c, even).wait_recv()
+            if even:
+                r.gbuf[c, :, :, x] = r.gbuf[c, :, :, x] + r.one_in[c]
+            else:
+                r.gbuf[c, :, y] = r.gbuf[c, :, y] + r.one_in[c]
+            stage_two(c, even).start()
+
+        by_parity(c, act)
+
+    x_small.wait()
+    r.total_x[...] = r.total[...] + r.x_small[...]
+    y_small = remote(r.total_x, r.y_small, r.misc_send.at[8], r.misc_recv.at[8], y_peer)
+    y_small.start()
+
+    @pl.loop(0, CHUNKS)
+    def _(c):
+        by_parity(c, lambda even: stage_two(c, even).wait_recv())
+        r.gbuf[c, :, y, x] = r.gbuf[c, :, y, x] + r.two_in[c]
+        for o in range(1, zs):
+            stage_three(c, o).start()
+
+    y_small.wait()
+    r.z_small[z] = r.total_x[...] + r.y_small[...]
+    z_sends = []
+    for o in range(1, zs):
+        z_sends.append(
+            remote(r.z_small.at[z], r.z_small.at[z], r.z_send.at[o], r.z_recv.at[z], z_peers[o - 1])
+        )
+        z_sends[-1].start()
+    ready("shard")
+    shard_swap.wait()
+    for copy in small1_swap:
+        copy.wait()
+    r.o_shard[1] = r.shard1[0] + r.shard_in[...]
+    r.o_small[9:26] = jnp.concatenate([r.small1[0:9], r.small1[12:20]], axis=0) + r.small1_in[...]
+
+    @pl.loop(0, CHUNKS)
+    def _(c):
+        total = r.gbuf[c, z, y, x].astype(F32)
+        for o in range(1, zs):
+            stage_three(c, o).wait_recv()
+            total = total + r.three_in[c, o - 1].astype(F32)
+        r.o_shard[0, c] = total
+
+    for o in range(1, zs):
+        source = lax.rem(z + o, zs)
+        remote(r.z_small.at[source], r.z_small.at[source], r.z_send.at[o], r.z_recv.at[source], z_peers[o - 1]).wait_recv()
+    total = r.z_small[0]
+    for k in range(1, zs):
+        total = total + r.z_small[k]
+    r.o_small[0:9] = total
+
+    for copy in z_sends:
+        copy.wait_send()
+
+    @pl.loop(0, CHUNKS)
+    def _(c):
+        def act(even):
+            stage_one(c, even).wait_send()
+            stage_two(c, even).wait_send()
+
+        by_parity(c, act)
+        for o in range(1, zs):
+            stage_three(c, o).wait_send()
+
+    for c in range(CHUNKS - SLOTS, CHUNKS):
+        sib_copy(jnp.int32(c)).wait_send()
+    grad_swap.wait()
+    enc_swap.wait()
+    for copy in outs:
+        copy.wait()
+
+
+def run_last(dp, rows, batches, cot, gain, dc, ret, small1, shard1, y1, saved, own, other):
+    hbm = pl.BlockSpec(memory_space=pl.ANY)
+    small = pl.BlockSpec(memory_space=pltpu.VMEM)
+    zs = dp // 4
+    shard = D // dp
+    outs = dict(
+        o_grad=((batches, rows, D), F32),
+        o_enc=((batches, rows, D), BF),
+        o_shard=((2, CHUNKS, shard, CHUNK), F32),
+        o_small=((26, 1, D), F32),
+    )
+    scratch = dict(saved_shapes(rows))
+    scratch.update(WEIGHT_SCRATCH)
+    scratch.update(BACK_SCRATCH)
+    scratch.update(
+        y1=((rows, D), BF),
+        cot=((rows, D), BF),
+        dr=((rows, D), F32),
+        dm=((rows, D), BF),
+        dmt=((D, rows), BF),
+        small=((12, 1, D), F32),
+        small_in=((9, 1, D), F32),
+        small1_in=((17, 1, D), F32),
+        total=((9, 1, D), F32),
+        total_x=((9, 1, D), F32),
+        x_small=((9, 1, D), F32),
+        y_small=((9, 1, D), F32),
+        z_small=((zs, 9, 1, D), F32),
+        shard1=((2, CHUNKS, shard, CHUNK), F32),
+        shard_in=((CHUNKS, shard, CHUNK), F32),
+        gbuf=((CHUNKS, zs, 2, 2, shard, CHUNK), BF),
+        sib_out=((SLOTS, D, CHUNK), BF),
+        sib_in=((SLOTS, D, CHUNK), BF),
+        one_in=((CHUNKS, zs, 2, shard, CHUNK), BF),
+        two_in=((CHUNKS, zs, shard, CHUNK), BF),
+        three_in=((CHUNKS, zs - 1, shard, CHUNK), BF),
+    )
+    dma = pltpu.SemaphoreType.DMA
+    sems = dict(
+        local_sem=dma((32,)),
+        misc_send=dma((9,)),
+        misc_recv=dma((9,)),
+        sib_send=dma((SLOTS,)),
+        sib_recv=dma((SLOTS,)),
+        one_send=dma((CHUNKS,)),
+        one_recv=dma((CHUNKS,)),
+        two_send=dma((CHUNKS,)),
+        two_recv=dma((CHUNKS,)),
+        three_send=dma((CHUNKS, zs - 1)),
+        three_recv=dma((CHUNKS, zs - 1)),
+        z_send=dma((zs,)),
+        z_recv=dma((zs,)),
+        credit=pltpu.SemaphoreType.REGULAR,
+    )
+    keys = list(saved_shapes(rows))
+    ins = ["i_cot", "gain", "dc", "ret", "small1", "i_shard1", "i_y1"] + ["i_" + k for k in keys]
+    ins += ["a_wqkv", "a_wout", "a_wup", "a_wdown", "x_wqkv", "x_wout", "x_wup", "x_wdown"]
+    names = ins + list(outs) + list(scratch) + list(sems)
+    result = pl.pallas_call(
+        partial(last_kernel, dp, names),
+        out_shape=arrays(outs),
+        in_specs=[hbm] + [small] * 4 + [hbm] * (2 + len(keys) + 8),
+        out_specs=[hbm, hbm, small, small],
+        scratch_shapes=vmem(scratch) + list(sems.values()),
+        compiler_params=pltpu.CompilerParams(
+            collective_id=1, has_side_effects=True, vmem_limit_bytes=63 << 20
+        ),
+        name="segment_backward",
+    )(cot, gain, dc, ret, small1, shard1, y1, *[saved[k] for k in keys], *own, *other)
+    return dict(zip(outs, result))
+
+
+def fused(tokens, seg_doc, doc_len, w_qkv, b_qv, w_out, w_up, b_up, w_down, norm_gain, bias_terms, seg_pos, cotangent):
+    batches, rows, width = tokens.shape
+    dp = lax.axis_size("dp")
+    segs = rows // SEG
+    slots = doc_len.shape[1] * MAXSEG
+    packed = jnp.concatenate([b_qv.reshape(2, 2 * HALF_D), b_up], axis=1).reshape(2, 1, PACK)
+    gain = norm_gain.reshape(2, 2, 1, D)
+    terms = bias_terms.reshape(2, 4, 1, D)
+    own = (w_qkv, w_out, w_up, w_down)
+    one = run_first(dp, rows, seg_doc, doc_len, tokens, cotangent, packed, gain[0], terms[0], *own)
+    other = tuple(one[k] for k in ("x_wqkv", "x_wout", "x_wup", "x_wdown"))
+    two = run_cross(
+        dp, segs, slots, seg_doc.reshape(2, 1, -1), one["o_cls"].reshape(dp * segs, D),
+        one["o_cot"].reshape(dp * segs, D), seg_pos, packed, one["o_packed"], gain[1], terms[1], own, other,
+    )
+    small1 = jnp.concatenate([two["small"], two["d_pos"].reshape(MAXSEG, 1, D)], axis=0)
+    three = run_last(
+        dp, rows, batches, cotangent, gain[0], two["dc"].reshape(8, 1, D), two["ret"].reshape(8, 1, D),
+        small1, two["shard"], one["o_y1"], {k: one["o_" + k] for k in saved_shapes(rows)}, own, other,
+    )
+    shard = three["o_shard"]
+    small = three["o_small"].reshape(26, D)
+    both = small[:18].reshape(2, 9, D)
+    shard_rows = D // dp
+    return (
+        three["o_enc"],
+        three["o_grad"],
+        shard[:, 9:12],
+        both[:, 6].reshape(2, 2, HALF_D),
+        shard[:, 8].transpose(0, 2, 1),
+        shard[:, 4:8].transpose(0, 2, 1, 3).reshape(2, shard_rows, HALF_FF),
+        both[:, 7:9].reshape(2, HALF_FF),
+        shard[:, 0:4].transpose(0, 1, 3, 2).reshape(2, HALF_FF, shard_rows),
+        both[:, 0:2],
+        both[:, 2:6],
+        small[18:26],
+    )
+
+
 def solution(mesh):
     in_specs = (
         P(None, "dp", None),
@@ -419,4 +1421,5 @@
         P(),
         P(),
     )
-    return jax.shard_map(local, mesh=mesh, in_specs=in_specs, out_specs=out_specs, check_vma=False)
+    body = fused if mesh.shape["dp"] == 16 and mesh.shape["tensor"] == 2 else local
+    return jax.shard_map(body, mesh=mesh, in_specs=in_specs, out_specs=out_specs, check_vma=False)

time: 1410 us -> 206 us (0.15)
  waiting for transfers between devices: 830 us -> 0 us
  blocking collectives: 195 us -> 0 us
  Pallas kernels: 0 us -> 176 us
  matrix products: 148 us -> 0 us
  other arithmetic: 96.4 us -> 2.16 us
  local copies, waits for them, and re-layouts: 103 us -> 26 us
  between operations: 21.4 us -> 0.71 us
    unnamed x22 -> x0, waiting for transfers between devices: 560 us -> none
    all_gather x14 -> x0, blocking collectives: 179 us -> none  [the longest x2 81.2 us: local(): lax.all_gather(cross_out.astype(jnp.bfloat16), 'dp', axis=0, tiled=True)]
    pallas_call x0 -> x3, Pallas kernels: none -> 176 us  [the longest x1 105 us: run_last(): pl.pallas_call(partial(last_kernel, dp, names), out_shape=arrays(outs), i...]
    dot_general x80 -> x0, matrix products: 148 us -> none  [the longest x4 27.1 us: layer_forward(): pre_act = jnp.dot(hidden_b, w_up, preferred_element_type=jnp.float32) + b_up]
    reduce_scatter x11 -> x0, waiting for transfers between devices: 136 us -> none  [the longest x2 115 us: local(): lax.psum_scatter(spreader(src_slot, grad_returned, slot_rows * lax.axis_s...]
    psum x1 -> x0, waiting for transfers between devices: 106 us -> none  [local(): lax.psum((jnp.stack([seg_total[1], cross_total[1]]), jnp.stack([seg_total...]
    another operation x63 -> x1, local copies, waits for them, and re-layouts: 44.1 us -> 0.61 us  [fused(): both[:, 6].reshape(2, 2, HALF_D)]
    reduce_sum x53 -> x0, other arithmetic: 42.4 us -> none  [the longest x12 14.8 us: norm_rows(): centre = values - jnp.mean(values, axis=-1, keepdims=True)]
  transfers between devices with their start and end apart: 20 -> 0, of which waited for: 9 -> 0; matrix products, arithmetic and copies ran while one was open for 14% -> 0% of each run, Pallas kernels for 0% -> 0%
where the time goes in v1:
time: 206 us; the launch traced here: 205 us
  Pallas kernels  176 us (85%)
  local copies, waits for them, and re-layouts  26 us (13%)
  other arithmetic  2.16 us (1%)
    pallas_call x1, Pallas kernels, run_last(): pl.pallas_call(partial(last_kernel, dp, names), out_shape=arrays(outs), i...  105 us
    pallas_call x1, Pallas kernels, run_first(): pl.pallas_call(partial(first_kernel, dp, names), out_shape=arrays(outs),...  45.3 us
    pallas_call x1, Pallas kernels, run_cross(): pl.pallas_call(kernel, out_shape=arrays(outs), in_specs=[small] * 8 + [hb...  25.8 us
    unnamed x10, local copies, waits for them, and re-layouts  7.36 us

profile of v1, /device:TPU:0, one launch (start us, length us, event | category | flops | bytes accessed | tf_op | source)
XLA Modules:
  0.0 204.9 jit_solution(12611801111751482353)
XLA Ops:
  0.6 0.7 copy.44
  1.3 0.7 pad_maximum_fusion.1
  2.1 0.6 reshape.74.refs_4_
  2.7 0.7 fusion.2
  3.4 0.6 copy_bitcast_fusion.3
  4.0 0.7 fusion.1
  4.7 0.6 copy_bitcast_fusion.1
  5.4 45.3 %segment_forward.1 = (bf16[2,3,768,384]{3,2,1,0:T(8,128)(2,1)}, bf16[2,384,768]{2,1,0:T(8,128)(2,1)}, bf16[2,768,1536]{2,1,0:T(8,128)(2,1)}, bf16[2,1536,768]{2,...) custom-call(s32[2,64]{1,0:T(2,128)} %refs_0_.2, ...), custom_call_target="tpu_custom_call" | custom-call | tf_op jit(solution)/shard_map/segment_forward/pallas_call | solution.py:888
  50.7 1.6 reshape.75.refs_1_
  52.2 1.6 reshape.76.refs_2_
  53.8 25.8 %document_layer.1 = (f32[8,768]{1,0:T(8,128)}, f32[8,768]{1,0:T(8,128)}, f32[8,768]{1,0:T(8,128)}, f32[12,1,768]{2,1,0:T(1,128)}, f32[2,12,48,384]{3,2,1,0:T(8,128)}) custom-call(s32[2,1,64]{2,1,0:T(1,128)} %bitcast.37, bf16[64,768]{1,0:T(8,128)(2,1)} %reshape.75.refs_1_, bf16[64,768]{1,0:T(8,128)(2,1)} %reshape.76.refs_2_, f32[8,768]{1,0:T(8,128)} %refs_3_.3, ...), custom_call_target="tpu_custom_call" | custom-call | tf_op jit(solution)/shard_map/document_layer/pallas_call | solution.py:1022
  79.6 1.4 reshape.77.refs_2_
  81.0 1.4 reshape.78.refs_3_
  82.3 0.8 reshape.79
  83.1 1.4 pad_maximum_fusion.refs_4_
  84.5 105.0 %segment_backward.1 = (f32[2,512,768]{2,1,0:T(8,128)}, bf16[2,512,768]{2,1,0:T(8,128)(2,1)}, f32[2,12,48,384]{3,2,1,0:T(8,128)}, f32[26,1,768]{2,1,0:T(1,128)}) custom-call(bf16[2,512,768]{2,1,0:T(8,128)(2,1)} %refs_0_.3, f32[2,1,768]{2,1,0:T(1,128)} %get-tuple-element.76.refs_5_.refs_1_, f32[8,1,768]{2,1,0:T(1,128)} %reshape.77.refs_2_, ...), custom_call_target="tpu_custom_call" | custom-call | tf_op jit(solution)/shard_map/segment_backward/pallas_call | solution.py:1342
  189.5 0.7 slice.64
  190.2 1.0 slice_reduce_fusion
  191.2 0.6 copy.51
  191.9 0.6 reshape_squeeze.3
  192.5 0.6 slice.69
  193.1 0.6 fusion
  193.7 0.6 copy.45
  194.3 1.6 slice_bitcast_fusion.2
  195.9 1.8 slice.55
  197.7 1.3 slice_bitcast_fusion
  199.0 0.0 copy-start.1
  199.0 0.9 copy.43
  199.9 0.9 copy.42
  200.8 0.0 copy-start
  200.8 0.0 copy-done.1
  200.8 1.1 copy.54
  201.9 1.3 copy-done
  203.2 1.7 copy.55
  (2 shorter events, 0.0 us)
Async XLA Ops:
  199.0 1.8 copy-start.1
  200.8 2.5 %copy-start = (f32[2,512,768]{2,1,0:T(8,128)S(1)}, f32[2,512,768]{2,1,0:T(8,128)}, u32[]{:S(2)}) copy-start(f32[2,512,768]{2,1,0:T(8,128)} %get-tuple-element.91) | copy-start | bytes 9437188

commit v2 on v0

--- a/solution.py
+++ b/solution.py
@@ -1,8 +1,10 @@
-from functools import reduce
+from functools import partial, reduce
 
 import jax
 import jax.numpy as jnp
 from jax import lax
+from jax.experimental import pallas as pl
+from jax.experimental.pallas import tpu as pltpu
 from jax.sharding import PartitionSpec as P
 
 HEAD_DIM = 64
@@ -390,6 +392,1188 @@
     )
 
 
+BF = jnp.bfloat16
+F32 = jnp.float32
+D = 768
+FF = 3072
+HALF_FF = FF // 2
+HALF_D = D // 2
+CHUNK = 384
+CHUNKS = 12
+PAIRS = 6
+MESH = pl.DeviceIdType.MESH
+ROOT_HALF = 0.7071067811865476
+PDF_SCALE = 0.3989422804014327
+
+
+class Names:
+    def __init__(self, **kw):
+        self.__dict__.update(kw)
+
+
+def mm(left, right):
+    return jnp.dot(left, right, preferred_element_type=F32)
+
+
+def mm_nt(left, right):
+    return lax.dot_general(left, right, (((1,), (1,)), ((), ())), preferred_element_type=F32)
+
+
+def span(index, size):
+    return pl.ds(pl.multiple_of(index * size, size), size)
+
+
+def row_norm(rows):
+    centre = rows - jnp.mean(rows, axis=-1, keepdims=True)
+    spread = jnp.mean(centre * centre, axis=-1, keepdims=True)
+    scale = lax.rsqrt(spread + norm_eps)
+    return centre * scale, scale
+
+
+def stacked(pair, low_half):
+    zero = jnp.zeros_like(pair)
+    return jnp.concatenate(
+        [jnp.where(low_half, pair, zero), jnp.where(low_half, zero, pair)], axis=0
+    )
+
+
+def soft_rows(scores):
+    top = jnp.max(scores, axis=-1, keepdims=True)
+    grown = jnp.exp(scores - top)
+    return (grown * (1.0 / jnp.sum(grown, axis=-1, keepdims=True))).astype(BF)
+
+
+def transpose_into(dest, source, rows):
+    @pl.loop(0, rows // SEG)
+    def _(s):
+        dest[:, span(s, SEG)] = source[span(s, SEG), :].T
+
+
+def gelu_pair(u):
+    cdf = 0.5 * (1.0 + lax.erf(u * ROOT_HALF))
+    slope = cdf + u * (PDF_SCALE * jnp.exp(-0.5 * u * u))
+    return (u * cdf).astype(BF), slope.astype(BF)
+
+
+def project(r):
+    @pl.loop(0, 9)
+    def _(i):
+        c = lax.div(i, 3)
+        cols = span(lax.rem(i, 3), 256)
+        r.qkv[c, :, cols] = (mm(r.xb[...], r.wqkv[c, :, cols]) + r.b3[c, :, cols]).astype(BF)
+
+
+def attend(r, keep):
+    @pl.loop(0, r.xb.shape[0] // SEG)
+    def _(s):
+        at = span(s, SEG)
+        live = keep(s)
+        low_half = lax.broadcasted_iota(jnp.int32, (SEG, SEG), 1) < HEAD_DIM
+        for p in range(PAIRS):
+            cols = slice(p * SEG, p * SEG + SEG)
+            keys = stacked(r.qkv[1, at, cols], low_half)
+            vals = stacked(r.qkv[2, at, cols], low_half)
+            raw = mm_nt(r.qkv[0, at, cols], keys) * HEAD_DIM ** (-0.5)
+            one = soft_rows(jnp.where(live, raw[:, :SEG], masked_score))
+            two = soft_rows(jnp.where(live, raw[:, SEG:], masked_score))
+            both = jnp.concatenate([one, two], axis=1)
+            r.p[s, p] = both
+            r.o[at, cols] = mm(both, vals).astype(BF)
+
+
+def attn_out(r):
+    @pl.loop(0, 3)
+    def _(n):
+        cols = span(n, 256)
+        r.xh1[:, cols] = mm(r.o[...], r.wout[:, cols]) + r.bt[0, :, cols]
+
+
+def norm_one(r):
+    @pl.loop(0, r.xb.shape[0] // 64)
+    def _(s):
+        at = span(s, 64)
+        hat, scale = row_norm(r.x_rows(at) + r.xh1[at, :])
+        r.xh1[at, :] = hat
+        r.rs1[at, :] = jnp.broadcast_to(scale, (64, SEG))
+        hidden = hat * r.gain[0] + r.bt[2]
+        r.h1[at, :] = hidden
+        r.h1b[at, :] = hidden.astype(BF)
+
+
+def mlp_up(r):
+    @pl.loop(0, 12)
+    def _(j):
+        cols = span(j, 256)
+        for b in range(r.xb.shape[0] // SEG):
+            at = slice(b * SEG, b * SEG + SEG)
+            u = mm(r.h1b[at, :], r.wup[:, cols]) + r.bup[:, cols]
+            r.g[at, cols], r.gp[at, cols] = gelu_pair(u)
+
+
+def mlp_down(r):
+    @pl.loop(0, 3)
+    def _(n):
+        cols = span(n, 256)
+        r.xh2[:, cols] = r.h1[:, cols] + mm(r.g[...], r.wdown[:, cols]) + r.bt[1, :, cols]
+
+
+def norm_two(r, y_block):
+    @pl.loop(0, r.xb.shape[0] // 64)
+    def _(s):
+        at = span(s, 64)
+        hat, scale = row_norm(r.xh2[at, :])
+        r.xh2[at, :] = hat
+        r.rs2[at, :] = jnp.broadcast_to(scale, (64, SEG))
+        y_block(at, hat * r.gain[1] + r.bt[3])
+
+
+def core_forward(r, keep, ready, y_block):
+    ready("qkv")
+    project(r)
+    attend(r, keep)
+    ready("out")
+    attn_out(r)
+    norm_one(r)
+    ready("up")
+    mlp_up(r)
+    transpose_into(r.h1t, r.h1b, r.xb.shape[0])
+    ready("down")
+    mlp_down(r)
+    norm_two(r, y_block)
+
+
+def norm_back(grad, hat, scale, gain):
+    d_hat = grad * gain
+    first = jnp.mean(d_hat, axis=-1, keepdims=True)
+    second = jnp.mean(d_hat * hat, axis=-1, keepdims=True)
+    return (d_hat - first - hat * second) * scale
+
+
+def norm_back_rows(r, rows, hat_ref, scale_ref, gain, grad_of):
+    zero = jnp.zeros((1, D), F32)
+
+    def step(s, sums):
+        at = span(s, 64)
+        grad = grad_of(s, at)
+        hat = hat_ref[at, :]
+        out = norm_back(grad, hat, scale_ref[at, 0:1], gain)
+        low = out.astype(BF)
+        r.dr[at, :] = out
+        r.dm[at, :] = low
+        return (
+            sums[0] + jnp.sum(grad * hat, axis=0, keepdims=True),
+            sums[1] + jnp.sum(grad, axis=0, keepdims=True),
+            sums[2] + jnp.sum(low.astype(F32), axis=0, keepdims=True),
+        )
+
+    sums = lax.fori_loop(0, rows // 64, step, (zero, zero, zero))
+    transpose_into(r.dmt, r.dm, rows)
+    return sums
+
+
+def grad_hidden(r):
+    @pl.loop(0, 12)
+    def _(j):
+        cols = span(j, 256)
+        du = (mm_nt(r.dm[...], r.wdown[cols, :]) * r.gp[:, cols].astype(F32)).astype(BF)
+        r.gp[:, cols] = du
+        r.bup_sum[:, cols] = jnp.sum(du.astype(F32), axis=0, keepdims=True)
+
+
+def grad_middle(r):
+    @pl.loop(0, 3)
+    def _(n):
+        cols = span(n, 256)
+        r.dr[:, cols] = r.dr[:, cols] + mm_nt(r.gp[...], r.wup[cols, :])
+
+
+def grad_heads(r):
+    @pl.loop(0, 3)
+    def _(n):
+        cols = span(n, 256)
+        r.o[:, cols] = mm_nt(r.dm[...], r.wout[cols, :]).astype(BF)
+
+
+def attend_back(r, between=None):
+    segs = r.dr.shape[0] // SEG
+    step = segs if between is None else 1
+    for low in range(0, segs, step):
+        attend_back_part(r, low, low + step)
+        if between is not None:
+            between(low)
+
+
+def attend_back_part(r, low, high):
+    @pl.loop(low, high)
+    def _(s):
+        at = span(s, SEG)
+        low_half = lax.broadcasted_iota(jnp.int32, (SEG, SEG), 1) < HEAD_DIM
+        scale = HEAD_DIM ** (-0.5)
+        for p in range(PAIRS):
+            cols = slice(p * SEG, p * SEG + SEG)
+            query = r.qkv[0, at, cols]
+            keys = stacked(r.qkv[1, at, cols], low_half)
+            vals = stacked(r.qkv[2, at, cols], low_half)
+            d_head = r.o[at, cols]
+            probs = r.p[s, p]
+            d_probs = mm_nt(d_head, vals)
+            d_vals = mm(probs.T, d_head)
+            wide = probs.astype(F32)
+            prod = wide * d_probs
+            parts = []
+            for h in range(2):
+                own = slice(h * SEG, h * SEG + SEG)
+                parts.append(
+                    prod[:, own]
+                    - wide[:, own] * jnp.sum(prod[:, own], axis=-1, keepdims=True)
+                )
+            d_scores = jnp.concatenate(parts, axis=1).astype(BF)
+            d_keys = mm(d_scores.T, query) * scale
+            r.qkv[0, at, cols] = (mm(d_scores, keys) * scale).astype(BF)
+            r.qkv[1, at, cols] = jnp.where(low_half, d_keys[:SEG], d_keys[SEG:]).astype(BF)
+            r.qkv[2, at, cols] = jnp.where(low_half, d_vals[:SEG], d_vals[SEG:]).astype(BF)
+
+
+def bias_heads(r):
+    for c in (0, 2):
+        r.qv_sum[c // 2] = jnp.sum(r.qkv[c].astype(F32), axis=0, keepdims=True)
+
+
+def grad_input(r):
+    @pl.loop(0, 3)
+    def _(n):
+        cols = span(n, 256)
+        total = r.dr[:, cols]
+        for c in range(3):
+            total = total + mm_nt(r.qkv[c], r.wqkv[c, cols, :])
+        r.dr[:, cols] = total
+
+
+def back_norm_two(r, grad_of):
+    sums = norm_back_rows(r, r.dr.shape[0], r.xh2, r.rs2, r.gain[1], grad_of)
+    r.small_common[1], r.small_common[5], r.small_common[3] = sums
+
+
+def back_norm_one(r):
+    sums = norm_back_rows(r, r.dr.shape[0], r.xh1, r.rs1, r.gain[0], lambda s, at: r.dr[at, :])
+    r.small_common[0], r.small_common[4], r.small_common[2] = sums
+
+
+def chunk_operands(r, c):
+    if c < 4:
+        return r.dmt, (r.g, c * CHUNK, HALF_FF + c * CHUNK)
+    if c < 8:
+        return r.h1t, (r.gp, (c - 4) * CHUNK, HALF_FF + (c - 4) * CHUNK)
+    if c == 8:
+        return r.dmt, (r.o, 0, HALF_D)
+    return r.xt, (r.qkv.at[c - 9], 0, HALF_D)
+
+
+HOOK_CHUNKS = {"down": (0, 4), "up": (4, 8), "out": (8, 9), "qkv": (9, 12)}
+
+
+class Copies:
+    def __init__(self, sems):
+        self.sems = sems
+        self.used = 0
+
+    def start(self, source, dest):
+        copy = pltpu.make_async_copy(source, dest, self.sems.at[self.used])
+        self.used += 1
+        copy.start()
+        return copy
+
+
+def remote(source, dest, send_sem, recv_sem, device):
+    return pltpu.make_async_remote_copy(
+        src_ref=source,
+        dst_ref=dest,
+        send_sem=send_sem,
+        recv_sem=recv_sem,
+        device_id=device,
+        device_id_type=MESH,
+    )
+
+
+class Gather:
+    def __init__(self, dp, everyone, send, recv):
+        self.dp, self.everyone, self.send, self.recv = dp, everyone, send, recv
+        self.sends = []
+
+    def start(self, block):
+        d, t = lax.axis_index("dp"), lax.axis_index("tensor")
+        everyone = self.everyone
+        everyone[d] = block
+        for o in range(1, self.dp):
+            peer = (lax.rem(d + o, self.dp), t)
+            copy = remote(everyone.at[d], everyone.at[d], self.send.at[o], self.recv.at[d], peer)
+            copy.start()
+            self.sends.append(copy)
+
+    def arrived(self):
+        d, t = lax.axis_index("dp"), lax.axis_index("tensor")
+        for o in range(1, self.dp):
+            source = lax.rem(d + o, self.dp)
+            block = self.everyone.at[source]
+            remote(block, block, self.send.at[o], self.recv.at[source], (source, t)).wait_recv()
+
+    def rows_into(self, dest):
+        segs = self.everyone.shape[1]
+        pack = 8 // segs
+        for i in range(self.dp // pack):
+            blocks = [self.everyone[i * pack + k].astype(F32) for k in range(pack)]
+            dest[i * 8 : i * 8 + 8, :] = jnp.concatenate(blocks, axis=0)
+
+
+SLOTS = 3
+RING = 8
+WEIGHTS = ("wqkv", "wout", "wup", "wdown")
+
+
+def half_of(ref, which, half):
+    if which == "wqkv":
+        return ref.at[:, :, half * HALF_D : (half + 1) * HALF_D]
+    if which == "wout":
+        return ref.at[half * HALF_D : (half + 1) * HALF_D, :]
+    if which == "wup":
+        return ref.at[:, half * HALF_FF : (half + 1) * HALF_FF]
+    return ref.at[half * HALF_FF : (half + 1) * HALF_FF, :]
+
+
+def fill_bias(b3, bup, half, layer, b_qv, b_up):
+    lanes = slice(half * HALF_D, (half + 1) * HALF_D)
+    b3[0, :, lanes] = b_qv[layer, 0:1, :]
+    b3[1, :, lanes] = jnp.zeros((1, HALF_D), F32)
+    b3[2, :, lanes] = b_qv[layer, 1:2, :]
+    bup[:, half * HALF_FF : (half + 1) * HALF_FF] = b_up[layer : layer + 1, :]
+
+
+def pack_halves(r):
+    for half in range(2):
+        at = 6 + 3 * half
+        lanes = slice(half * HALF_D, (half + 1) * HALF_D)
+        r.small[at, :, 0:HALF_D] = r.qv_sum[0, :, lanes]
+        r.small[at, :, HALF_D:] = r.qv_sum[1, :, lanes]
+        base = half * HALF_FF
+        r.small[at + 1] = r.bup_sum[:, base : base + D]
+        r.small[at + 2] = r.bup_sum[:, base + D : base + 2 * D]
+
+
+def first_of_segments(ref, segs):
+    return jnp.concatenate(
+        [ref[s * SEG : s * SEG + 16, :].astype(F32)[0:1] for s in range(segs)], axis=0
+    )
+
+
+class Stream:
+    COUNTS = {"qkv": 9, "out": 3, "up": 12, "down": 12}
+
+    def __init__(self, r):
+        self.r = r
+
+    def parts(self, phase, j, act):
+        r = self.r
+        which = "w" + phase
+        own, other = getattr(r, "a_" + which).at[1], getattr(r, "f_" + which)
+        buffer, sems = (r.wide, r.wide_sem) if phase in ("qkv", "up") else (r.tall, r.tall_sem)
+        slot = lax.rem(j, 3)
+        half = (HALF_D if phase in ("qkv", "out") else HALF_FF) // SEG
+        for k in range(2):
+            if phase == "qkv":
+                c, block = lax.div(j, 3), 2 * lax.rem(j, 3) + k
+            else:
+                c, block = None, 2 * j + k
+
+            def source(ref, at):
+                if phase == "qkv":
+                    return ref.at[c, :, span(at, SEG)]
+                return ref.at[:, span(at, SEG)] if phase == "up" else ref.at[span(at, SEG), :]
+
+            lanes = slice(k * SEG, k * SEG + SEG)
+            if phase in ("qkv", "up"):
+                dest = buffer.at[slot, :, lanes]
+            else:
+                dest = buffer.at[slot, lanes, :]
+            sem = sems.at[slot, k]
+            if act == "wait":
+                pltpu.make_async_copy(source(other, 0), dest, sem).wait()
+                continue
+
+            @pl.when(block < half)
+            def _():
+                pltpu.make_async_copy(source(own, block), dest, sem).start()
+
+            @pl.when(block >= half)
+            def _():
+                pltpu.make_async_copy(source(other, block - half), dest, sem).start()
+
+    def prime(self, phase):
+        for j in range(3):
+            self.parts(phase, jnp.int32(j), "start")
+
+    def run(self, phase, body):
+        buffer = self.r.wide if phase in ("qkv", "up") else self.r.tall
+        count = self.COUNTS[phase]
+
+        @pl.loop(0, count)
+        def _(j):
+            self.parts(phase, j, "wait")
+            body(j, buffer.at[lax.rem(j, 3)])
+
+            @pl.when(j + 3 < count)
+            def _():
+                self.parts(phase, j + 3, "start")
+
+
+def cross_layer(r, q, stream, keep, pump, hooks):
+    slots = q.xb.shape[0]
+
+    def project_piece(j, w):
+        c = lax.div(j, 3)
+        cols = span(lax.rem(j, 3), 256)
+        q.qkv[c, :, cols] = (mm(q.xb[...], w[...]) + q.b3[c, :, cols]).astype(BF)
+
+    stream.run("qkv", project_piece)
+    stream.prime("up")
+    attend(q, keep)
+    pump("attend")
+    q.xh1[...] = jnp.broadcast_to(q.bt[0], (slots, D))
+
+    def out_piece(j, w):
+        q.xh1[...] = q.xh1[...] + mm(q.o[:, span(j, 256)], w[...])
+
+    stream.run("out", out_piece)
+    stream.prime("down")
+    norm_one(q)
+    transpose_into(q.h1t, q.h1b, slots)
+
+    def up_piece(j, w):
+        cols = span(j, 256)
+        u = mm(q.h1b[...], w[...]) + q.bup[:, cols]
+        act, slope = gelu_pair(u)
+        q.g[:, cols] = act
+        q.gp[:, cols] = slope
+
+    stream.run("up", up_piece)
+    stream.prime("up")
+    pump("up")
+    q.xh2[...] = q.h1[...] + q.bt[1]
+
+    def down_piece(j, w):
+        q.xh2[...] = q.xh2[...] + mm(q.g[:, span(j, 256)], w[...])
+
+    stream.run("down", down_piece)
+    stream.prime("down")
+
+    def y_block(at, values):
+        q.yb[at, :] = values.astype(BF)
+
+    norm_two(q, y_block)
+    pump("down")
+    back_norm_two(q, lambda s, at: q.dy[at, :])
+    hooks("down")
+
+    def back_down_piece(j, w):
+        cols = span(j, 256)
+        du = (mm_nt(q.dm[...], w[...]) * q.gp[:, cols].astype(F32)).astype(BF)
+        q.gp[:, cols] = du
+        r.bup_sum[:, cols] = jnp.sum(du.astype(F32), axis=0, keepdims=True)
+
+    stream.run("down", back_down_piece)
+    stream.prime("out")
+    pump("back_down")
+    hooks("up")
+
+    def back_up_piece(j, w):
+        q.dr[...] = q.dr[...] + mm_nt(q.gp[:, span(j, 256)], w[...])
+
+    stream.run("up", back_up_piece)
+    stream.prime("qkv")
+    pump("back_up")
+    back_norm_one(q)
+    hooks("out")
+
+    def back_out_piece(j, w):
+        q.o[:, span(j, 256)] = mm_nt(q.dm[...], w[...]).astype(BF)
+
+    stream.run("out", back_out_piece)
+    attend_back(q)
+    bias_heads(q)
+    pump("attend_back")
+    hooks("qkv")
+
+    def back_qkv_piece(j, w):
+        q.dr[...] = q.dr[...] + mm_nt(q.qkv[lax.div(j, 3), :, span(lax.rem(j, 3), 256)], w[...])
+
+    stream.run("qkv", back_qkv_piece)
+
+
+def whole_kernel(dp, names, *refs):
+    r = Names(**dict(zip(names, refs)))
+    d, t = lax.axis_index("dp"), lax.axis_index("tensor")
+    x, y, z = lax.rem(d, 2), lax.rem(lax.div(d, 2), 2), lax.div(d, 4)
+    zs = dp // 4
+    shard = D // dp
+    rows = r.xb.shape[0]
+    segs = rows // SEG
+    sibling = (d, 1 - t)
+    x_peer = (z * 4 + y * 2 + (1 - x), t)
+    y_peer = (z * 4 + (1 - y) * 2 + x, t)
+    z_peers = [(lax.rem(z + o, zs) * 4 + y * 2 + x, t) for o in range(1, zs)]
+    r.dr, r.dm, r.y1 = r.h1, r.h1b, r.xb
+
+    barrier = pltpu.get_barrier_semaphore()
+    for device in [sibling] + [(lax.rem(d + o, dp), t) for o in range(1, dp)]:
+        pl.semaphore_signal(barrier, inc=1, device_id=device, device_id_type=MESH)
+    copies = Copies(r.local_sem)
+    for layer, gain, terms in ((0, r.gain, r.bt), (1, r.gain_cross, r.bt_cross)):
+        for k in range(2):
+            gain[k] = r.norm_gain[layer, k : k + 1, :]
+        for k in range(4):
+            terms[k] = r.bias_terms[layer, k : k + 1, :]
+    own = {w: getattr(r, "a_" + w) for w in WEIGHTS}
+    full = {w: getattr(r, "f_" + w) for w in WEIGHTS}
+    load_x = copies.start(r.tokens.at[t], r.xb)
+    loads = {w: copies.start(own[w].at[0], half_of(getattr(r, w), w, 0)) for w in WEIGHTS}
+    load_cot = copies.start(r.cotangent.at[t], r.cot)
+    pl.semaphore_wait(barrier, dp)
+
+    swaps = {}
+
+    def swap(layer, w):
+        k = WEIGHTS.index(w)
+        dest = half_of(getattr(r, w), w, 1) if layer == 0 else full[w]
+        swaps[layer, w] = remote(
+            own[w].at[layer], dest, r.w_send.at[layer, k], r.w_recv.at[layer, k], sibling
+        )
+        swaps[layer, w].start()
+
+    swap(0, "wqkv")
+    swap_bias = [
+        remote(r.b_qv, r.x_bqv, r.w_send.at[0, 4], r.w_recv.at[0, 4], sibling),
+        remote(r.b_up, r.x_bup, r.w_send.at[1, 4], r.w_recv.at[1, 4], sibling),
+    ]
+    for copy in swap_bias:
+        copy.start()
+    swap(0, "wout")
+    cot_gather = Gather(dp, r.cot_all, r.g_send.at[0], r.g_recv.at[0])
+    cls_gather = Gather(dp, r.cls_all, r.g_send.at[1], r.g_recv.at[1])
+    hat_gather = Gather(dp, r.hat_all, r.g_send.at[2], r.g_recv.at[2])
+    act_gather = Gather(dp, r.act_all, r.g_send.at[3], r.g_recv.at[3])
+
+    def ready(phase):
+        if phase == "qkv":
+            load_x.wait()
+            transpose_into(r.xt, r.xb, rows)
+            fill_bias(r.b3, r.bup, 0, 0, r.b_qv, r.b_up)
+            fill_bias(r.b3_cross, r.bup_cross, 0, 1, r.b_qv, r.b_up)
+            load_cot.wait()
+            cot_gather.start(first_of_segments(r.cot, segs).astype(BF))
+            loads["wqkv"].wait()
+            swaps[0, "wqkv"].wait_recv()
+            swap(0, "wup")
+            swap(0, "wdown")
+            for copy in swap_bias:
+                copy.wait_recv()
+            fill_bias(r.b3, r.bup, 1, 0, r.x_bqv, r.x_bup)
+            fill_bias(r.b3_cross, r.bup_cross, 1, 1, r.x_bqv, r.x_bup)
+        else:
+            w = "w" + phase
+            loads[w].wait()
+            swaps[0, w].wait_recv()
+            if phase == "out":
+                swap(1, "wqkv")
+                swap(1, "wout")
+            elif phase == "up":
+                swap(1, "wup")
+                swap(1, "wdown")
+
+    def keep(s):
+        seg = d * segs + s
+        doc = r.seg_doc[t, seg]
+        within = jnp.int32(0)
+        for back in range(1, MAXSEG):
+            same = r.seg_doc[t, jnp.maximum(seg - back, 0)] == doc
+            within = within + jnp.where(jnp.logical_and(seg >= back, same), 1, 0)
+        valid = jnp.minimum(SEG, r.doc_len[t, doc] - SEG * within)
+        return lax.broadcasted_iota(jnp.int32, (1, SEG), 1) < valid
+
+    r.x_rows = lambda at: r.xb[at, :].astype(F32)
+
+    def y_block(at, values):
+        r.y1[at, :] = values.astype(BF)
+
+    core_forward(r, keep, ready, y_block)
+    cls_gather.start(first_of_segments(r.y1, segs).astype(BF))
+    hats = first_of_segments(r.xh2, segs)
+    hat_gather.start(jnp.concatenate([hats, first_of_segments(r.rs2, segs)], axis=1))
+    act_gather.start(first_of_segments(r.g, segs).astype(BF))
+
+    def sib_copy(c):
+        slot = lax.rem(c, SLOTS)
+        return remote(
+            r.sib_out.at[slot], r.sib_in.at[slot], r.sib_send.at[slot], r.sib_recv.at[slot], sibling
+        )
+
+    def ring(c):
+        return lax.rem(c, RING)
+
+    def stage_one(c, even):
+        g = r.gbuf.at[ring(c)]
+        source = g.at[:, :, 1 - x] if even else g.at[:, 1 - y]
+        return remote(source, r.one_in.at[ring(c)], r.one_send.at[c], r.one_recv.at[c], x_peer if even else y_peer)
+
+    def stage_two(c, even):
+        g = r.gbuf.at[ring(c)]
+        source = g.at[:, 1 - y, x] if even else g.at[:, y, 1 - x]
+        return remote(source, r.two_in.at[ring(c)], r.two_send.at[c], r.two_recv.at[c], y_peer if even else x_peer)
+
+    def stage_three(c, o):
+        return remote(
+            r.gbuf.at[ring(c), lax.rem(z + o, zs), y, x],
+            r.three_in.at[ring(c), o - 1],
+            r.three_send.at[c, o - 1],
+            r.three_recv.at[c, o - 1],
+            z_peers[o - 1],
+        )
+
+    def by_parity(c, act):
+        @pl.when(lax.rem(c, 2) == 0)
+        def _():
+            act(True)
+
+        @pl.when(lax.rem(c, 2) == 1)
+        def _():
+            act(False)
+
+    def progress(c):
+        sib_copy(c).wait_recv()
+        slot = lax.rem(c, SLOTS)
+        r.gbuf[ring(c)] = r.gbuf[ring(c)] + r.sib_in[slot].reshape(zs, 2, 2, shard, CHUNK)
+
+        @pl.when(c < CHUNKS - SLOTS)
+        def _():
+            pl.semaphore_signal(r.credit, inc=1, device_id=sibling, device_id_type=MESH)
+
+        by_parity(c, lambda even: stage_one(c, even).start())
+
+    def emit(c, left, right, own_at, other_at):
+        @pl.when(c >= SLOTS)
+        def _():
+            sib_copy(c).wait_send()
+            pl.semaphore_wait(r.credit, 1)
+
+        slot = lax.rem(c, SLOTS)
+        r.sib_out[slot] = mm(left[...], right[:, pl.ds(other_at, CHUNK)]).astype(BF)
+        sib_copy(c).start()
+        mine = mm(left[...], right[:, pl.ds(own_at, CHUNK)]).astype(BF)
+        r.gbuf[ring(c)] = mine.reshape(zs, 2, 2, shard, CHUNK)
+
+    def hooks(name):
+        low, high = HOOK_CHUNKS[name]
+
+        @pl.loop(low, high)
+        def _(c):
+            if name == "out":
+                emit(c, r.dmt, r.o, 0, HALF_D)
+            elif name == "qkv":
+                emit(c, r.xt, r.qkv.at[c - low], 0, HALF_D)
+            else:
+                base = pl.multiple_of((c - low) * CHUNK, 128)
+                left, right = (r.dmt, r.g) if name == "down" else (r.h1t, r.gp)
+                emit(c, left, right, base, pl.multiple_of(base + HALF_FF, 128))
+
+            @pl.when(c > low)
+            def _():
+                progress(c - 1)
+
+    def second(*chunks):
+        for c in chunks:
+            even = c % 2 == 0
+            c = jnp.int32(c)
+            stage_one(c, even).wait_recv()
+            if even:
+                r.gbuf[ring(c), :, :, x] = r.gbuf[ring(c), :, :, x] + r.one_in[ring(c)]
+            else:
+                r.gbuf[ring(c), :, y] = r.gbuf[ring(c), :, y] + r.one_in[ring(c)]
+            stage_two(c, even).start()
+
+    def third(*chunks):
+        for c in chunks:
+            even = c % 2 == 0
+            c = jnp.int32(c)
+            stage_two(c, even).wait_recv()
+            r.gbuf[ring(c), :, y, x] = r.gbuf[ring(c), :, y, x] + r.two_in[ring(c)]
+            for o in range(1, zs):
+                stage_three(c, o).start()
+
+    def finish(*chunks):
+        for c in chunks:
+            even = c % 2 == 0
+            at = jnp.int32(c)
+            total = r.gbuf[ring(at), z, y, x].astype(F32)
+            for o in range(1, zs):
+                stage_three(at, o).wait_recv()
+                total = total + r.three_in[ring(at), o - 1].astype(F32)
+            r.mine[c] = r.mine[c] + total if c < 4 else total
+            stage_one(at, even).wait_send()
+            stage_two(at, even).wait_send()
+            for o in range(1, zs):
+                stage_three(at, o).wait_send()
+
+    first_row = lax.broadcasted_iota(jnp.int32, (64, 1), 0)
+
+    def without_first(s, at):
+        row = first_row + 64 * lax.rem(s, segs * SEG // (segs * 64))
+        return jnp.where(row == 0, 0.0, r.cot[at, :].astype(F32))
+
+    r.small_common = r.small
+    back_norm_two(r, without_first)
+    hooks("down")
+
+    q = Names(
+        **{k: getattr(r, "q_" + k) for k in CROSS},
+        g=r.g.at[0:SEG],
+        gp=r.g.at[SEG : 2 * SEG],
+        gain=r.gain_cross,
+        bt=r.bt_cross,
+        b3=r.b3_cross,
+        bup=r.bup_cross,
+        qv_sum=r.qv_sum,
+    )
+    q.dr, q.dm, q.small_common = q.h1, q.h1b, r.small1
+    slots = q.xb.shape[0]
+    total_docs = slots // MAXSEG
+    total_segs = dp * segs
+    for w in WEIGHTS:
+        swaps[1, w].wait_recv()
+    stream = Stream(r)
+    stream.prime("qkv")
+    stream.prime("out")
+
+    doc = jnp.where(t == 0, r.seg_doc_v[0:1, :], r.seg_doc_v[1:2, :])
+    below = lax.broadcasted_iota(jnp.int32, (total_segs, total_segs), 0)
+    across = lax.broadcasted_iota(jnp.int32, (total_segs, total_segs), 1)
+
+    def column(row):
+        wide = jnp.broadcast_to(row, (total_segs, total_segs))
+        return jnp.sum(jnp.where(below == across, wide, 0.0), axis=1, keepdims=True)
+
+    doc_f = doc.astype(F32)
+    earlier = jnp.logical_and(column(doc_f) == doc_f, below < across)
+    within = jnp.sum(jnp.where(earlier, 1.0, 0.0), axis=0, keepdims=True).astype(jnp.int32)
+    moved = doc + total_docs // 2
+    moved = jnp.where(moved >= total_docs, moved - total_docs, moved)
+    slot_of = (jnp.where((doc & 1) == 1, moved, doc) * MAXSEG + within).astype(F32)
+    slot_ids = lax.broadcasted_iota(jnp.int32, (slots, total_segs), 0).astype(F32)
+    deal = jnp.where(slot_ids == slot_of, 1.0, 0.0).astype(BF)
+    slot_row = lax.broadcasted_iota(jnp.int32, (total_segs, slots), 1).astype(F32)
+    r.undeal[...] = jnp.where(slot_row == column(slot_of), 1.0, 0.0).astype(BF)
+    pick_row = lax.broadcasted_iota(jnp.int32, (8, total_segs), 0)
+    pick_seg = lax.broadcasted_iota(jnp.int32, (8, total_segs), 1)
+    picked = jnp.logical_and(pick_row < segs, pick_seg == d * segs + pick_row)
+    r.back[...] = mm(jnp.where(picked, 1.0, 0.0).astype(BF), r.undeal[...]).astype(BF)
+    live = mm_nt(jnp.ones((8, total_segs), BF), deal)[0:1] > 0.5
+    key_doc = lax.broadcasted_iota(jnp.int32, (SEG, SEG), 1) >> 3
+    row_doc = lax.broadcasted_iota(jnp.int32, (SEG, SEG), 0) >> 3
+    r.allowed[...] = jnp.where(jnp.logical_and(key_doc == row_doc, live), 1.0, 0.0)
+
+    cot_gather.arrived()
+    cot_gather.rows_into(r.rows64)
+    q.dy[...] = mm(deal, r.rows64[...].astype(BF))
+    cls_gather.arrived()
+    cls_gather.rows_into(r.rows64)
+    q.x32[...] = mm(deal, r.rows64[...].astype(BF)) + jnp.concatenate(
+        [r.seg_pos[...]] * total_docs, axis=0
+    )
+    q.xb[...] = q.x32[...].astype(BF)
+    q.x_rows = lambda at: q.x32[at, :]
+    transpose_into(q.xt, q.xb, slots)
+    progress(jnp.int32(3))
+
+    def cross_hooks(name):
+        low, high = HOOK_CHUNKS[name]
+        for c in range(low, high):
+            left, (right, own_at, other_at) = chunk_operands(q, c)
+            mine = left[pl.ds(pl.multiple_of(d * shard, 16), shard), :]
+            r.shard1[c] = mm(mine, right[:, own_at : own_at + CHUNK])
+            r.shard_out[c] = mm(mine, right[:, other_at : other_at + CHUNK]).astype(BF)
+
+    def pump(point):
+        if point == "up":
+            second(0, 1)
+        elif point == "back_down":
+            second(2, 3)
+        elif point == "attend_back":
+            third(0, 1)
+
+    cross_layer(r, q, stream, lambda s: r.allowed[...] > 0.5, pump, cross_hooks)
+    r.small, keep_small = r.small1, r.small
+    pack_halves(r)
+    r.small = keep_small
+    total = q.dr[0:MAXSEG, :]
+    for j in range(1, total_docs):
+        total = total + q.dr[j * MAXSEG : (j + 1) * MAXSEG, :]
+    for k in range(MAXSEG):
+        r.small1[12 + k] = total[k : k + 1, :]
+    r.ret[...] = mm(r.back[...], q.yb[...])
+    low = q.dr[...].astype(BF)
+    r.dc[...] = mm(r.back[...], low)
+
+    gain_sum = jnp.zeros((1, D), F32)
+    shift_sum, low_sum = gain_sum, gain_sum
+    top = lax.broadcasted_iota(jnp.int32, (16, 1), 0) == 0
+    for s in range(segs):
+        at = slice(s * SEG, s * SEG + 16)
+        grad = jnp.where(top, r.dc[s : s + 1, :], 0.0)
+        hat = r.xh2[at, :]
+        out = jnp.where(top, norm_back(grad, hat, r.rs2[at, 0:1], r.gain[1]), 0.0)
+        out_low = out.astype(BF)
+        r.dr[at, :] = jnp.where(top, out, r.dr[at, :])
+        r.dm[at, :] = jnp.where(top, out_low.astype(F32), r.dm[at, :].astype(F32)).astype(BF)
+        gain_sum = gain_sum + jnp.sum(grad * hat, axis=0, keepdims=True)
+        shift_sum = shift_sum + jnp.sum(grad, axis=0, keepdims=True)
+        low_sum = low_sum + jnp.sum(out_low.astype(F32), axis=0, keepdims=True)
+        r.y1[at, :] = jnp.where(top, r.ret[s : s + 1, :], r.y1[at, :].astype(F32)).astype(BF)
+    r.small_common[1] = r.small_common[1] + gain_sum
+    r.small_common[5] = r.small_common[5] + shift_sum
+    r.small_common[3] = r.small_common[3] + low_sum
+    outs = [copies.start(r.y1, r.o_enc.at[t])]
+    enc_swap = remote(r.y1, r.o_enc.at[t], r.misc_send.at[0], r.misc_recv.at[0], sibling)
+    enc_swap.start()
+
+    hat_gather.arrived()
+    hat_gather.rows_into(r.hat64)
+    act_gather.arrived()
+    act_gather.rows_into(r.act64)
+    all_grads = mm(r.undeal[...], low)
+    late = norm_back(all_grads, r.hat64[:, 0:D], r.hat64[:, D : D + 1], r.gain[1]).astype(BF)
+    r.late[0:total_segs, :] = late
+    r.late[total_segs:, :] = jnp.zeros((SEG - total_segs, D), BF)
+    transpose_into(r.late_t, r.late, SEG)
+    mine = r.late_t[pl.ds(pl.multiple_of(d * shard, 16), shard), 0:total_segs]
+    for c in range(4):
+        for half in range(2):
+            cols = slice(half * HALF_FF + c * CHUNK, half * HALF_FF + (c + 1) * CHUNK)
+            part = mm(mine, r.act64[:, cols].astype(BF))
+            if half == 0:
+                r.mine[c] = part
+            else:
+                r.shard_out[CHUNKS + c] = part.astype(BF)
+    cross_swap = [
+        remote(r.shard_out, r.shard_in, r.misc_send.at[1], r.misc_recv.at[1], sibling),
+        remote(r.small1.at[0:6], r.small1_in.at[0:6], r.misc_send.at[2], r.misc_recv.at[2], sibling),
+        remote(r.small1.at[9:20], r.small1_in.at[6:17], r.misc_send.at[3], r.misc_recv.at[3], sibling),
+    ]
+    for copy in cross_swap:
+        copy.start()
+
+    third(2, 3)
+    grad_hidden(r)
+    hooks("up")
+    grad_middle(r)
+    progress(jnp.int32(7))
+    for copy in cross_swap:
+        copy.wait()
+    finish(0, 1, 2, 3)
+    for c in range(CHUNKS):
+        r.shard1[c] = r.shard1[c] + r.shard_in[c].astype(F32)
+    for c in range(4):
+        r.mine[c] = r.mine[c] + r.shard_in[CHUNKS + c].astype(F32)
+    r.o_small[9:26] = (
+        jnp.concatenate([r.small1[0:9], r.small1[12:20]], axis=0) + r.small1_in[...]
+    )
+    outs.append(copies.start(r.shard1, r.o_shard.at[1]))
+    back_norm_one(r)
+    second(4)
+    hooks("out")
+    grad_heads(r)
+    progress(jnp.int32(8))
+
+    def between(s):
+        if s == 1:
+            second(5)
+        if s == 3:
+            second(6, 7)
+
+    attend_back(r, between)
+    bias_heads(r)
+    hooks("qkv")
+    pack_halves(r)
+    small_swap = [
+        remote(r.small.at[0:6], r.small_in.at[0:6], r.misc_send.at[4], r.misc_recv.at[4], sibling),
+        remote(r.small.at[9:12], r.small_in.at[6:9], r.misc_send.at[5], r.misc_recv.at[5], sibling),
+    ]
+    for copy in small_swap:
+        copy.start()
+    progress(jnp.int32(11))
+    third(4, 5)
+    grad_input(r)
+    grad_swap = remote(r.dr, r.o_grad.at[t], r.misc_send.at[6], r.misc_recv.at[6], sibling)
+    grad_swap.start()
+    outs.append(copies.start(r.dr, r.o_grad.at[t]))
+    for copy in small_swap:
+        copy.wait()
+    r.total[...] = r.small[0:9] + r.small_in[...]
+    x_small = remote(r.total, r.x_small, r.misc_send.at[7], r.misc_recv.at[7], x_peer)
+    x_small.start()
+    third(6, 7)
+    second(8)
+    x_small.wait()
+    r.total_x[...] = r.total[...] + r.x_small[...]
+    y_small = remote(r.total_x, r.y_small, r.misc_send.at[8], r.misc_recv.at[8], y_peer)
+    y_small.start()
+    second(9)
+    finish(4, 5, 6, 7)
+    y_small.wait()
+    r.z_small[z] = r.total_x[...] + r.y_small[...]
+    z_sends = []
+    for o in range(1, zs):
+        z_sends.append(
+            remote(r.z_small.at[z], r.z_small.at[z], r.z_send.at[o], r.z_recv.at[z], z_peers[o - 1])
+        )
+        z_sends[-1].start()
+    second(10, 11)
+    third(8, 9, 10, 11)
+    for o in range(1, zs):
+        source = lax.rem(z + o, zs)
+        block = r.z_small.at[source]
+        remote(block, block, r.z_send.at[o], r.z_recv.at[source], z_peers[o - 1]).wait_recv()
+    total = r.z_small[0]
+    for k in range(1, zs):
+        total = total + r.z_small[k]
+    r.o_small[0:9] = total
+    finish(8, 9, 10, 11)
+    outs.append(copies.start(r.mine, r.o_shard.at[0]))
+
+    for copy in z_sends:
+        copy.wait_send()
+    for c in range(CHUNKS - SLOTS, CHUNKS):
+        sib_copy(jnp.int32(c)).wait_send()
+    for gathered in (cot_gather, cls_gather, hat_gather, act_gather):
+        for copy in gathered.sends:
+            copy.wait_send()
+    for copy in swap_bias:
+        copy.wait_send()
+    for copy in swaps.values():
+        copy.wait_send()
+    grad_swap.wait()
+    enc_swap.wait()
+    for copy in outs:
+        copy.wait()
+
+
+CROSS = ("xb", "x32", "xt", "h1t", "h1b", "h1", "qkv", "o", "p", "xh1", "rs1", "xh2", "rs2", "yb", "dy", "dmt")
+WEIGHT_SCRATCH = dict(
+    wqkv=((3, D, D), BF), wout=((D, D), BF), wup=((D, FF), BF), wdown=((FF, D), BF)
+)
+BACK_SCRATCH = dict(qv_sum=((2, 1, D), F32), bup_sum=((1, FF), F32))
+
+
+def saved_shapes(rows):
+    return dict(
+        xt=((D, rows), BF),
+        h1t=((D, rows), BF),
+        qkv=((3, rows, D), BF),
+        o=((rows, D), BF),
+        p=((rows // SEG, PAIRS, SEG, 2 * SEG), BF),
+        xh1=((rows, D), F32),
+        rs1=((rows, SEG), F32),
+        g=((rows, FF), BF),
+        gp=((rows, FF), BF),
+        xh2=((rows, D), F32),
+        rs2=((rows, SEG), F32),
+    )
+
+
+def forward_shapes(rows):
+    return dict(
+        xb=((rows, D), BF),
+        h1=((rows, D), F32),
+        h1b=((rows, D), BF),
+        b3=((3, 1, D), F32),
+        bup=((1, FF), F32),
+    )
+
+
+def vmem(table):
+    return [pltpu.VMEM(shape, kind) for shape, kind in table.values()]
+
+
+def arrays(table):
+    return [jax.ShapeDtypeStruct(shape, kind) for shape, kind in table.values()]
+
+
+def run_whole(dp, inputs):
+    hbm = pl.BlockSpec(memory_space=pl.ANY)
+    small = pl.BlockSpec(memory_space=pltpu.VMEM)
+    smem = pl.BlockSpec(memory_space=pltpu.SMEM)
+    batches, rows, _ = inputs["tokens"].shape
+    slots = inputs["doc_len"].shape[1] * MAXSEG
+    segs = rows // SEG
+    total_segs = dp * segs
+    zs = dp // 4
+    shard = D // dp
+    outs = dict(
+        o_enc=((batches, rows, D), BF),
+        o_grad=((batches, rows, D), F32),
+        o_shard=((2, CHUNKS, shard, CHUNK), F32),
+        o_small=((26, 1, D), F32),
+    )
+    outs.update({"f_" + w: (inputs["a_" + w].shape[1:], BF) for w in WEIGHTS})
+    scratch = dict(saved_shapes(rows))
+    scratch.update(WEIGHT_SCRATCH)
+    scratch.update(forward_shapes(rows))
+    scratch.update(BACK_SCRATCH)
+    cross = dict(saved_shapes(slots))
+    cross.update(forward_shapes(slots))
+    cross.update(
+        x32=((slots, D), F32), yb=((slots, D), BF), dy=((slots, D), F32), dmt=((D, slots), BF)
+    )
+    scratch.update({"q_" + k: cross[k] for k in CROSS})
+    scratch.update(
+        b3_cross=((3, 1, D), F32),
+        bup_cross=((1, FF), F32),
+        gain=((2, 1, D), F32),
+        gain_cross=((2, 1, D), F32),
+        bt=((4, 1, D), F32),
+        bt_cross=((4, 1, D), F32),
+        x_bqv=((2, 2, HALF_D), F32),
+        x_bup=((2, HALF_FF), F32),
+        cot=((rows, D), BF),
+        dmt=((D, rows), BF),
+        wide=((3, D, 256), BF),
+        tall=((3, 256, D), BF),
+        cot_all=((dp, segs, D), BF),
+        cls_all=((dp, segs, D), BF),
+        hat_all=((dp, segs, D + SEG), F32),
+        act_all=((dp, segs, FF), BF),
+        rows64=((total_segs, D), F32),
+        hat64=((total_segs, D + SEG), F32),
+        act64=((total_segs, FF), F32),
+        undeal=((total_segs, slots), BF),
+        back=((8, slots), BF),
+        allowed=((SEG, SEG), F32),
+        ret=((8, D), F32),
+        dc=((8, D), F32),
+        late=((SEG, D), BF),
+        late_t=((D, SEG), BF),
+        small=((12, 1, D), F32),
+        small1=((20, 1, D), F32),
+        small_in=((9, 1, D), F32),
+        small1_in=((17, 1, D), F32),
+        total=((9, 1, D), F32),
+        total_x=((9, 1, D), F32),
+        x_small=((9, 1, D), F32),
+        y_small=((9, 1, D), F32),
+        z_small=((zs, 9, 1, D), F32),
+        shard1=((CHUNKS, shard, CHUNK), F32),
+        shard_out=((CHUNKS + 4, shard, CHUNK), BF),
+        shard_in=((CHUNKS + 4, shard, CHUNK), BF),
+        mine=((CHUNKS, shard, CHUNK), F32),
+        gbuf=((RING, zs, 2, 2, shard, CHUNK), BF),
+        sib_out=((SLOTS, D, CHUNK), BF),
+        sib_in=((SLOTS, D, CHUNK), BF),
+        one_in=((RING, zs, 2, shard, CHUNK), BF),
+        two_in=((RING, zs, shard, CHUNK), BF),
+        three_in=((RING, zs - 1, shard, CHUNK), BF),
+    )
+    dma = pltpu.SemaphoreType.DMA
+    sems = dict(
+        local_sem=dma((20,)),
+        w_send=dma((2, 5)),
+        w_recv=dma((2, 5)),
+        wide_sem=dma((3, 2)),
+        tall_sem=dma((3, 2)),
+        g_send=dma((4, dp)),
+        g_recv=dma((4, dp)),
+        misc_send=dma((9,)),
+        misc_recv=dma((9,)),
+        sib_send=dma((SLOTS,)),
+        sib_recv=dma((SLOTS,)),
+        one_send=dma((CHUNKS,)),
+        one_recv=dma((CHUNKS,)),
+        two_send=dma((CHUNKS,)),
+        two_recv=dma((CHUNKS,)),
+        three_send=dma((CHUNKS, zs - 1)),
+        three_recv=dma((CHUNKS, zs - 1)),
+        z_send=dma((zs,)),
+        z_recv=dma((zs,)),
+        credit=pltpu.SemaphoreType.REGULAR,
+    )
+    ins = dict(
+        seg_doc=smem, doc_len=smem, seg_doc_v=small, tokens=hbm, cotangent=hbm, b_qv=small, b_up=small,
+        norm_gain=small, bias_terms=small, seg_pos=small,
+        a_wqkv=hbm, a_wout=hbm, a_wup=hbm, a_wdown=hbm,
+    )
+    names = list(ins) + list(outs) + list(scratch) + list(sems)
+    result = pl.pallas_call(
+        partial(whole_kernel, dp, names),
+        out_shape=arrays(outs),
+        in_specs=list(ins.values()),
+        out_specs=[hbm, hbm, hbm, small] + [hbm] * 4,
+        scratch_shapes=vmem(scratch) + list(sems.values()),
+        compiler_params=pltpu.CompilerParams(
+            collective_id=0, has_side_effects=True, vmem_limit_bytes=VMEM_LIMIT
+        ),
+        name="both_layers",
+    )(*[inputs[k] for k in ins])
+    return dict(zip(outs, result))
+
+
+VMEM_LIMIT = 64 << 20
+
+
+def finish_kernel(shard, small, g_qkv, g_bqv, g_out, g_up, g_bup, g_down, g_gain, g_terms, g_pos):
+    for layer in range(2):
+        at = 9 * layer
+        for c in range(4):
+            g_down[layer, :, c * CHUNK : (c + 1) * CHUNK] = shard[layer, c]
+            g_up[layer, :, c * CHUNK : (c + 1) * CHUNK] = shard[layer, 4 + c]
+        g_out[layer] = shard[layer, 8]
+        for c in range(3):
+            g_qkv[layer, c] = shard[layer, 9 + c]
+        for k in range(2):
+            g_gain[layer, k : k + 1, :] = small[at + k]
+            g_bqv[layer, k : k + 1, :] = small[at + 6, :, k * HALF_D : (k + 1) * HALF_D]
+            g_bup[layer : layer + 1, k * D : (k + 1) * D] = small[at + 7 + k]
+        for k in range(4):
+            g_terms[layer, k : k + 1, :] = small[at + 2 + k]
+    for k in range(MAXSEG):
+        g_pos[k : k + 1, :] = small[18 + k]
+
+
+def fused(tokens, seg_doc, doc_len, w_qkv, b_qv, w_out, w_up, b_up, w_down, norm_gain, bias_terms, seg_pos, cotangent):
+    dp = lax.axis_size("dp")
+    whole = run_whole(
+        dp,
+        dict(
+            seg_doc=seg_doc, doc_len=doc_len, seg_doc_v=seg_doc, tokens=tokens, cotangent=cotangent,
+            b_qv=b_qv, b_up=b_up, norm_gain=norm_gain, bias_terms=bias_terms,
+            seg_pos=seg_pos, a_wqkv=w_qkv, a_wout=w_out, a_wup=w_up, a_wdown=w_down,
+        ),
+    )
+    rows = D // dp
+    shapes = [
+        (2, 3, rows, HALF_D), (2, 2, HALF_D), (2, rows, HALF_D), (2, rows, HALF_FF), (2, HALF_FF),
+        (2, rows, HALF_FF), (2, 2, D), (2, 4, D), (MAXSEG, D),
+    ]
+    small = pl.BlockSpec(memory_space=pltpu.VMEM)
+    grads = pl.pallas_call(
+        finish_kernel,
+        out_shape=[jax.ShapeDtypeStruct(shape, F32) for shape in shapes],
+        in_specs=[small] * 2,
+        out_specs=[small] * len(shapes),
+        compiler_params=pltpu.CompilerParams(vmem_limit_bytes=32 << 20),
+        name="lay_out",
+    )(whole["o_shard"], whole["o_small"])
+    g_qkv, g_bqv, g_out, g_up, g_bup, g_down, g_gain, g_terms, g_pos = grads
+    return (
+        whole["o_enc"], whole["o_grad"], g_qkv, g_bqv, g_out.transpose(0, 2, 1), g_up, g_bup,
+        g_down.transpose(0, 2, 1), g_gain, g_terms, g_pos,
+    )
+
+
 def solution(mesh):
     in_specs = (
         P(None, "dp", None),
@@ -419,4 +1603,5 @@
         P(),
         P(),
     )
-    return jax.shard_map(local, mesh=mesh, in_specs=in_specs, out_specs=out_specs, check_vma=False)
+    body = fused if mesh.shape["dp"] == 16 and mesh.shape["tensor"] == 2 else local
+    return jax.shard_map(body, mesh=mesh, in_specs=in_specs, out_specs=out_specs, check_vma=False)

time: 1410 us -> 151 us (0.11)
  waiting for transfers between devices: 830 us -> 0 us
  blocking collectives: 195 us -> 0 us
  matrix products: 148 us -> 0 us
  Pallas kernels: 0 us -> 143 us
  other arithmetic: 96.4 us -> 0 us
  local copies, waits for them, and re-layouts: 103 us -> 6.94 us
  between operations: 21.4 us -> 0.67 us
    unnamed x22 -> x0, waiting for transfers between devices: 560 us -> none
    all_gather x14 -> x0, blocking collectives: 179 us -> none  [the longest x2 81.2 us: local(): lax.all_gather(cross_out.astype(jnp.bfloat16), 'dp', axis=0, tiled=True)]
    dot_general x80 -> x0, matrix products: 148 us -> none  [the longest x4 27.1 us: layer_forward(): pre_act = jnp.dot(hidden_b, w_up, preferred_element_type=jnp.float32) + b_up]
    pallas_call x0 -> x2, Pallas kernels: none -> 143 us  [the longest x1 141 us: run_whole(): pl.pallas_call(partial(whole_kernel, dp, names), out_shape=arrays(outs),...]
    reduce_scatter x11 -> x0, waiting for transfers between devices: 136 us -> none  [the longest x2 115 us: local(): lax.psum_scatter(spreader(src_slot, grad_returned, slot_rows * lax.axis_s...]
    psum x1 -> x0, waiting for transfers between devices: 106 us -> none  [local(): lax.psum((jnp.stack([seg_total[1], cross_total[1]]), jnp.stack([seg_total...]
    another operation x63 -> x0, local copies, waits for them, and re-layouts: 44.1 us -> none  [the longest x1 15.2 us: local(): jnp.stack([seg_total[5], cross_total[5]])]
    reduce_sum x53 -> x0, other arithmetic: 42.4 us -> none  [the longest x12 14.8 us: norm_rows(): centre = values - jnp.mean(values, axis=-1, keepdims=True)]
  transfers between devices with their start and end apart: 20 -> 0, of which waited for: 9 -> 0; matrix products, arithmetic and copies ran while one was open for 14% -> 0% of each run, Pallas kernels for 0% -> 0%
where the time goes in v2:
time: 151 us; the launch traced here: 150 us
  Pallas kernels  143 us (95%)
  local copies, waits for them, and re-layouts  6.94 us (5%)
    pallas_call x1, Pallas kernels, run_whole(): pl.pallas_call(partial(whole_kernel, dp, names), out_shape=arrays(outs),...  141 us
    unnamed x8, local copies, waits for them, and re-layouts  6.94 us

profile of v2, /device:TPU:0, one launch (start us, length us, event | category | flops | bytes accessed | tf_op | source)
XLA Modules:
  0.0 150.2 jit_solution(7626111272736108409)
XLA Ops:
  0.6 141.3 %both_layers.1 = (bf16[2,512,768]{2,1,0:T(8,128)(2,1)}, f32[2,512,768]{2,1,0:T(8,128)}, f32[2,12,48,384]{3,2,1,0:T(8,128)}, f32[26,1,768]{2,1,0:T(1,128)}, bf16[...) custom-call(s32[2,64]{1,0:T(2,128)} %refs_2_.1, ...), custom_call_target="tpu_custom_call" | custom-call | tf_op jit(solution)/shard_map/both_layers/pallas_call | solution.py:1510
  141.9 0.0 copy-start
  141.9 1.5 copy-done
  143.4 0.0 copy-start.1
  143.4 0.9 copy-done.1
  144.3 0.0 copy-start.2
  144.3 1.3 lay_out.1
  145.6 2.9 %copy.26 = bf16[2,512,768]{2,1,0:T(8,128)(2,1)} copy(bf16[2,512,768]{2,1,0:T(8,128)(2,1)} %get-tuple-element.48) | data formatting | bytes 3145728
  148.6 0.0 copy-done.2
  148.6 1.7 %copy.27 = f32[2,512,768]{2,1,0:T(8,128)} copy(f32[2,512,768]{2,1,0:T(8,128)S(1)} %copy-done.2) | data formatting | bytes 6291456
Async XLA Ops:
  141.9 1.5 copy-start
  143.4 0.9 copy-start.1
  144.3 4.3 %copy-start.2 = (f32[2,512,768]{2,1,0:T(8,128)S(1)}, f32[2,512,768]{2,1,0:T(8,128)}, u32[]{:S(2)}) copy-start(f32[2,512,768]{2,1,0:T(8,128)} %get-tuple-element.49) | copy-start | bytes 9437188
